TPU v7x, 32 devices: a whole 2x2x4 slice. The times are simulated.
32 devices in a mesh: groups: 2 (over x), probe: 16 (over z, y, core).
Axes of the slice: x: 2, y: 2, z: 4, core: 2. Of those that a mesh axis runs over, the one named last changes fastest.
Arguments:
- atom_positions: float32 [2, 32768], P(None, ('groups', 'probe')), parts along dimension 1, may hold values from 0 to 512
- atom_species: int32 [32768], P(('groups', 'probe')), parts along dimension 0, may hold values from 0 to 7
- atom_slice: int32 [32768], P(('groups', 'probe')), parts along dimension 0, may hold values from 0 to 3
- species_amp: float32 [8], replicated, may hold values from 0.02 to 0.125
- species_width: float32 [8], replicated, may hold values from 2 to 8
- probe_spectrum: float32 [2, 256, 256], replicated, may hold values from -6 to 6
- window_offsets: int32 [128, 2], P(('groups', 'probe')), parts along dimension 0, may hold values from 0 to 256
- probe_shifts: int32 [128, 2], P(('groups', 'probe')), parts along dimension 0, may hold values from 0 to 255
- slice_phase: float32 [3], replicated, may hold values from 0.0002746582 to 0.001373291
Outputs:
- scan_spectrum: float32 [2, 128, 65536], P(None, 'groups', 'probe'), parts along dimension 1
There are 2 independent parts, one for each index of `groups`. A program takes and returns all parts, laid end to end along the dimension named above; an argument that names none is the same for every part. Nothing has to cross between parts.
All inputs are finite; a program needn't handle non-finite values.
Results may differ from a plain program's by a relative error of at most 0.025.
Values may be sent and summed in bfloat16 or wider, within the bound.
No kernel may reach another device: no remote copies, remote signals or barrier semaphores. Data moves between devices by JAX's collectives and lax.ppermute only.
A program may use at most 64 MiB of HBM per device.

v0:
```python
import math

import jax
import jax.numpy as jnp
from jax import lax
from jax.sharding import PartitionSpec as P

G = 512
W = 256
SLICES = 4


def dft_tables(length):
    indices = jnp.arange(length, dtype=jnp.int32)
    angles = (
        2.0 * math.pi / length * (indices[:, None] * indices[None, :] % length).astype(jnp.float32)
    )
    factor = 1.0 / math.sqrt(length)
    return (
        (jnp.cos(angles) * factor).astype(jnp.bfloat16),
        (jnp.sin(angles) * factor).astype(jnp.bfloat16),
    )


def along_rows(real_part, imag_part, matrix, direction):
    batch_count = real_part.shape[0]
    length = real_part.shape[1]
    stacked = jnp.concatenate([real_part, imag_part], axis=0)
    product = jnp.einsum("ky,byx->bkx", matrix, stacked, preferred_element_type=jnp.float32)
    new_real = product[:batch_count, :length] - direction * product[batch_count:, length:]
    new_imag = product[batch_count:, :length] + direction * product[:batch_count, length:]
    return (new_real, new_imag)


def along_columns(real_part, imag_part, matrix, direction):
    batch_count = real_part.shape[0]
    length = real_part.shape[2]
    stacked = jnp.concatenate([real_part, imag_part], axis=0)
    product = jnp.einsum("byx,xl->byl", stacked, matrix, preferred_element_type=jnp.float32)
    new_real = product[:batch_count, :, :length] - direction * product[batch_count:, :, length:]
    new_imag = product[batch_count:, :, :length] + direction * product[:batch_count, :, length:]
    return (new_real, new_imag)


def transmit(real_part, imag_part, window):
    values = window.astype(jnp.float32)
    cosine = jnp.cos(values)
    sine = jnp.sin(values)
    return (
        (real_part * cosine - imag_part * sine).astype(jnp.bfloat16),
        (real_part * sine + imag_part * cosine).astype(jnp.bfloat16),
    )


def frequencies(length):
    indices = jnp.arange(length, dtype=jnp.int32)
    frequency = (indices + length // 2) % length - length // 2
    squared = frequency[:, None] * frequency[:, None] + frequency[None, :] * frequency[None, :]
    aperture = (9 * squared < length * length).astype(jnp.float32)
    return (squared.astype(jnp.float32), aperture)


def multislice(probe_spectrum, shifts, windows, slice_phase):
    length = probe_spectrum.shape[-1]
    cos_table, sin_table = dft_tables(length)
    rows_matrix = jnp.concatenate([cos_table, sin_table], axis=0)
    columns_matrix = jnp.concatenate([cos_table, sin_table], axis=1)
    squared, aperture = frequencies(length)
    indices = jnp.arange(length, dtype=jnp.int32)
    phase_index = (
        indices[None, :, None] * shifts[:, 0][:, None, None]
        + indices[None, None, :] * shifts[:, 1][:, None, None]
    ) % length
    angles = 2.0 * math.pi / length * phase_index.astype(jnp.float32)
    cosine = jnp.cos(angles)
    sine = jnp.sin(angles)
    real_part = (probe_spectrum[0] * cosine + probe_spectrum[1] * sine).astype(jnp.bfloat16)
    imag_part = (probe_spectrum[1] * cosine - probe_spectrum[0] * sine).astype(jnp.bfloat16)
    real_part, imag_part = along_rows(real_part, imag_part, rows_matrix, 1.0)
    real_part, imag_part = along_columns(
        real_part.astype(jnp.bfloat16), imag_part.astype(jnp.bfloat16), columns_matrix, 1.0
    )
    real_part, imag_part = transmit(real_part, imag_part, windows[0])
    for layer in range(len(windows) - 1):
        real_part, imag_part = along_rows(real_part, imag_part, rows_matrix, -1.0)
        real_part, imag_part = along_columns(
            real_part.astype(jnp.bfloat16), imag_part.astype(jnp.bfloat16), columns_matrix, -1.0
        )
        phases = slice_phase[layer] * squared
        prop_real = aperture * jnp.cos(phases)
        prop_imag = -aperture * jnp.sin(phases)
        new_real = (real_part * prop_real - imag_part * prop_imag).astype(jnp.bfloat16)
        new_imag = (real_part * prop_imag + imag_part * prop_real).astype(jnp.bfloat16)
        real_part, imag_part = along_rows(new_real, new_imag, rows_matrix, 1.0)
        real_part, imag_part = along_columns(
            real_part.astype(jnp.bfloat16), imag_part.astype(jnp.bfloat16), columns_matrix, 1.0
        )
        real_part, imag_part = transmit(real_part, imag_part, windows[layer + 1])
    real_part, imag_part = along_rows(real_part, imag_part, rows_matrix, -1.0)
    real_part, imag_part = along_columns(
        real_part.astype(jnp.bfloat16), imag_part.astype(jnp.bfloat16), columns_matrix, -1.0
    )
    return (aperture * (real_part * real_part + imag_part * imag_part)).astype(jnp.bfloat16)


def atom_factors(
    atom_positions, atom_species, atom_slice, species_amp, species_width, grid, layers
):
    species_ids = jnp.arange(species_amp.shape[0], dtype=jnp.int32)
    selector = (atom_species[:, None] == species_ids[None, :]).astype(jnp.float32)
    amplitude = jnp.sum(selector * species_amp[None, :], axis=1)
    widths = jnp.sum(selector * species_width[None, :], axis=1)
    inverse_spread = 0.5 / (widths * widths)
    pixels = jnp.arange(grid, dtype=jnp.float32)
    along_y = jnp.exp(
        -jnp.square(pixels[:, None] - atom_positions[0][None, :]) * inverse_spread[None, :]
    )
    layer_ids = jnp.arange(layers, dtype=jnp.int32)
    weight = amplitude[None, :] * (atom_slice[None, :] == layer_ids[:, None]).astype(jnp.float32)
    row_factor = (
        (weight[:, None, :] * along_y[None, :, :]).astype(jnp.bfloat16).reshape(layers * grid, -1)
    )
    column_factor = jnp.exp(
        -jnp.square(pixels[None, :] - atom_positions[1][:, None]) * inverse_spread[:, None]
    ).astype(jnp.bfloat16)
    return (row_factor, column_factor)


def scan_transform(received):
    intensity = received[:, 0, :]
    positions = intensity.shape[0]
    cos_scan, sin_scan = dft_tables(positions)
    matrix = jnp.concatenate([cos_scan, sin_scan], axis=0)
    product = jnp.dot(matrix, intensity, preferred_element_type=jnp.float32)
    return jnp.stack([product[:positions], -product[positions:]], axis=0)


def on_device(
    atom_positions,
    atom_species,
    atom_slice,
    species_amp,
    species_width,
    probe_spectrum,
    window_offsets,
    probe_shifts,
    slice_phase,
):
    devices = lax.axis_size("probe")
    row_factor, column_factor = atom_factors(
        atom_positions, atom_species, atom_slice, species_amp, species_width, G, SLICES
    )
    partial_field = jnp.dot(row_factor, column_factor, preferred_element_type=jnp.float32)
    whole_field = lax.psum(partial_field, "probe").astype(jnp.bfloat16).reshape(SLICES, G, G)
    slabs = [whole_field[layer] for layer in range(SLICES)]
    windows = []
    for slab in slabs:
        windows.append(
            jax.vmap(lambda corner: lax.dynamic_slice(slab, (corner[0], corner[1]), (W, W)))(
                window_offsets
            )
        )
    intensity = multislice(probe_spectrum, probe_shifts, windows, slice_phase)
    local_count = intensity.shape[0]
    pieces = intensity.reshape(local_count, devices, W * W // devices)
    return scan_transform(lax.all_to_all(pieces, "probe", split_axis=1, concat_axis=0, tiled=True))


def solution(mesh):
    placed = (
        P(None, ("groups", "probe")),
        P(("groups", "probe")),
        P(("groups", "probe")),
        P(),
        P(),
        P(),
        P(("groups", "probe"), None),
        P(("groups", "probe"), None),
        P(),
    )
    return jax.shard_map(
        on_device, mesh=mesh, in_specs=placed, out_specs=P(None, "groups", "probe"), check_vma=False
    )
```

profile of v0, /device:TPU:0, one launch (start us, length us, event | category | flops | bytes accessed | tf_op | source)
XLA Modules:
  0.0 217.3 jit_solution(16012172392962101634)
XLA Ops:
  0.0 1.1 multiply_convert_fusion.1
  1.1 0.8 select_reduce_fusion.1
  1.9 0.8 fusion.193
  3.2 0.7 fusion.167
  3.9 1.1 multiply_convert_fusion
  5.0 4.6 %fusion.16 = f32[2048,512]{1,0:T(8,128)} fusion(bf16[2048,1024]{1,0:T(8,128)(2,1)S(1)} %bitcast.101, f32[1024]{0:T(1024)S(1)} %multiply_divide_fusion, f32[1024]{0:T(1024)S(1)} %bitcast.104), kind=kOutput, calls=%fused_computation.49 | convolution fusion | flops 2150105088 | bytes 8396800 | tf_op jit(solution)/shard_map/dot_general | solution.py:153
  9.5 97.1 %all-reduce.1 = bf16[2048,512]{1,0:T(8,128)(2,1)S(1)} all-reduce(f32[2048,512]{1,0:T(8,128)} %fusion.16), channel_id=1, replica_groups=mesh['groups'=2,'probe'=16] {'probe'}, use_global_device_ids=true, to_apply=%region_2.0 | all-reduce | flops 1048576 | bytes 6291456 | tf_op jit(solution)/shard_map/psum | solution.py:154
  106.6 1.2 fusion.192
  107.8 11.6 %while.7 = (s32[]{:T(128)}, bf16[512,512]{1,0:T(8,128)(2,1)}, s32[4,2]{0,1:T(2,128)S(1)}, bf16[4,256,256]{2,1,0:T(8,128)(2,1)S(1)}, s32[]{:T(128)}) while((s32[]{:T(128)}, bf16[512,512]{1,0:T(8,128)(2,1)}, s32[4,2]{0,1:T(2,128)S(1)}, bf16[4,256,256]{2,1,0:T(8,128)(2,1)S(1)}, s32[]{:T(128)}) %tuple.96), condition=%wide.while_cond.3, body=%wide.while_body.3.sunk | while | flops 2 | bytes 262261 | solution.py:159
  107.9 0.5 fusion.204
  108.5 2.2 %bitcast_dynamic-update-slice_fusion.11 = bf16[4,256,256]{2,1,0:T(8,128)(2,1)S(1)} fusion(bf16[4,256,256]{2,1,0:T(8,128)(2,1)S(1)} %get-tuple-element.264, s32[]{:T(128)S(6)} %copy.159, bf16[512,512]{1,0:T(8,128)(2,1)} %get-tuple-element.267, s32[]{:T(128)} %bitcast.99, s32[]{:T(128)} %bitcast.100), kind=kLoop, calls=%fused_computation.6.clone.1 | loop fusion | bytes 262156 | tf_op jit(solution)/shard_map/vmap()/gather
  110.8 0.5 fusion.204
  111.4 2.2 %bitcast_dynamic-update-slice_fusion.11 = bf16[4,256,256]{2,1,0:T(8,128)(2,1)S(1)} fusion(bf16[4,256,256]{2,1,0:T(8,128)(2,1)S(1)} %get-tuple-element.264, s32[]{:T(128)S(6)} %copy.159, bf16[512,512]{1,0:T(8,128)(2,1)} %get-tuple-element.267, s32[]{:T(128)} %bitcast.99, s32[]{:T(128)} %bitcast.100), kind=kLoop, calls=%fused_computation.6.clone.1 | loop fusion | bytes 262156 | tf_op jit(solution)/shard_map/vmap()/gather
  113.7 0.5 fusion.204
  114.3 2.2 %bitcast_dynamic-update-slice_fusion.11 = bf16[4,256,256]{2,1,0:T(8,128)(2,1)S(1)} fusion(bf16[4,256,256]{2,1,0:T(8,128)(2,1)S(1)} %get-tuple-element.264, s32[]{:T(128)S(6)} %copy.159, bf16[512,512]{1,0:T(8,128)(2,1)} %get-tuple-element.267, s32[]{:T(128)} %bitcast.99, s32[]{:T(128)} %bitcast.100), kind=kLoop, calls=%fused_computation.6.clone.1 | loop fusion | bytes 262156 | tf_op jit(solution)/shard_map/vmap()/gather
  116.6 0.5 fusion.204
  117.1 2.2 %bitcast_dynamic-update-slice_fusion.11 = bf16[4,256,256]{2,1,0:T(8,128)(2,1)S(1)} fusion(bf16[4,256,256]{2,1,0:T(8,128)(2,1)S(1)} %get-tuple-element.264, s32[]{:T(128)S(6)} %copy.159, bf16[512,512]{1,0:T(8,128)(2,1)} %get-tuple-element.267, s32[]{:T(128)} %bitcast.99, s32[]{:T(128)} %bitcast.100), kind=kLoop, calls=%fused_computation.6.clone.1 | loop fusion | bytes 262156 | tf_op jit(solution)/shard_map/vmap()/gather
  119.4 0.7 fusion.194
  120.1 11.9 %while.6 = (s32[]{:T(128)}, bf16[512,512]{1,0:T(8,128)(2,1)}, s32[4,2]{0,1:T(2,128)S(1)}, bf16[4,256,256]{2,1,0:T(8,128)(2,1)S(1)}, s32[]{:T(128)}) while((s32[]{:T(128)}, bf16[512,512]{1,0:T(8,128)(2,1)}, s32[4,2]{0,1:T(2,128)S(1)}, bf16[4,256,256]{2,1,0:T(8,128)(2,1)S(1)}, s32[]{:T(128)}) %tuple.108), condition=%wide.while_cond.2, body=%wide.while_body.2.sunk | while | flops 2 | bytes 262261 | solution.py:159
  120.2 0.6 fusion.203
  120.8 2.3 %bitcast_dynamic-update-slice_fusion.10 = bf16[4,256,256]{2,1,0:T(8,128)(2,1)S(1)} fusion(bf16[4,256,256]{2,1,0:T(8,128)(2,1)S(1)} %get-tuple-element.279, s32[]{:T(128)S(6)} %copy.165, bf16[512,512]{1,0:T(8,128)(2,1)} %get-tuple-element.282, s32[]{:T(128)} %bitcast.96, s32[]{:T(128)} %bitcast.97), kind=kLoop, calls=%fused_computation.4.clone.1 | loop fusion | bytes 262156 | tf_op jit(solution)/shard_map/vmap()/gather
  123.2 0.6 fusion.203
  123.8 2.3 %bitcast_dynamic-update-slice_fusion.10 = bf16[4,256,256]{2,1,0:T(8,128)(2,1)S(1)} fusion(bf16[4,256,256]{2,1,0:T(8,128)(2,1)S(1)} %get-tuple-element.279, s32[]{:T(128)S(6)} %copy.165, bf16[512,512]{1,0:T(8,128)(2,1)} %get-tuple-element.282, s32[]{:T(128)} %bitcast.96, s32[]{:T(128)} %bitcast.97), kind=kLoop, calls=%fused_computation.4.clone.1 | loop fusion | bytes 262156 | tf_op jit(solution)/shard_map/vmap()/gather
  126.1 0.6 fusion.203
  126.7 2.3 %bitcast_dynamic-update-slice_fusion.10 = bf16[4,256,256]{2,1,0:T(8,128)(2,1)S(1)} fusion(bf16[4,256,256]{2,1,0:T(8,128)(2,1)S(1)} %get-tuple-element.279, s32[]{:T(128)S(6)} %copy.165, bf16[512,512]{1,0:T(8,128)(2,1)} %get-tuple-element.282, s32[]{:T(128)} %bitcast.96, s32[]{:T(128)} %bitcast.97), kind=kLoop, calls=%fused_computation.4.clone.1 | loop fusion | bytes 262156 | tf_op jit(solution)/shard_map/vmap()/gather
  129.1 0.6 fusion.203
  129.7 2.3 %bitcast_dynamic-update-slice_fusion.10 = bf16[4,256,256]{2,1,0:T(8,128)(2,1)S(1)} fusion(bf16[4,256,256]{2,1,0:T(8,128)(2,1)S(1)} %get-tuple-element.279, s32[]{:T(128)S(6)} %copy.165, bf16[512,512]{1,0:T(8,128)(2,1)} %get-tuple-element.282, s32[]{:T(128)} %bitcast.96, s32[]{:T(128)} %bitcast.97), kind=kLoop, calls=%fused_computation.4.clone.1 | loop fusion | bytes 262156 | tf_op jit(solution)/shard_map/vmap()/gather
  132.0 7.8 %while.5 = (s32[]{:T(128)}, bf16[512,512]{1,0:T(8,128)(2,1)S(1)}, s32[4,2]{0,1:T(2,128)S(1)}, bf16[4,256,256]{2,1,0:T(8,128)(2,1)S(1)}, s32[]{:T(128)}) while((s32[]{:T(128)}, bf16[512,512]{1,0:T(8,128)(2,1)S(1)}, s32[4,2]{0,1:T(2,128)S(1)}, bf16[4,256,256]{2,1,0:T(8,128)(2,1)S(1)}, s32[]{:T(128)}) %tuple.109), condition=%wide.while_cond.1, body=%wide.while_body.1.sunk | while | flops 2 | bytes 262261 | solution.py:159
  132.6 1.3 bitcast_dynamic-update-slice_fusion.9
  134.6 1.3 bitcast_dynamic-update-slice_fusion.9
  136.5 1.3 bitcast_dynamic-update-slice_fusion.9
  138.5 1.3 bitcast_dynamic-update-slice_fusion.9
  139.9 7.8 %while.4 = (s32[]{:T(128)}, bf16[512,512]{1,0:T(8,128)(2,1)S(1)}, s32[4,2]{0,1:T(2,128)S(1)}, bf16[4,256,256]{2,1,0:T(8,128)(2,1)S(1)}, s32[]{:T(128)}) while((s32[]{:T(128)}, bf16[512,512]{1,0:T(8,128)(2,1)S(1)}, s32[4,2]{0,1:T(2,128)S(1)}, bf16[4,256,256]{2,1,0:T(8,128)(2,1)S(1)}, s32[]{:T(128)}) %tuple.110), condition=%wide.while_cond, body=%wide.while_body.sunk | while | flops 2 | bytes 262261 | solution.py:159
  140.5 1.3 bitcast_dynamic-update-slice_fusion.8
  142.4 1.3 bitcast_dynamic-update-slice_fusion.8
  144.4 1.3 bitcast_dynamic-update-slice_fusion.8
  146.3 1.3 bitcast_dynamic-update-slice_fusion.8
  147.7 1.1 slice_bitcast_fusion.2
  149.1 4.8 %add_convert_fusion.3 = (bf16[4,256,256]{1,2,0:T(8,128)(2,1)S(1)}, bf16[4,256,256]{1,2,0:T(8,128)(2,1)S(1)}) fusion(f32[256,256]{0,1:T(8,128)S(1)} %copy.105, s32[4,256]{1,0:T(4,128)S(1)} %get-tuple-element.134, s32[4,256]{1,0:T(4,128)S(1)} %get-tuple-element.135, f32[256,256]{0,1:T(8,128)S(1)} %copy.104), kind=kLoop, calls=%fused_computation.206 | loop fusion | flops 5767168 | bytes 1581056 | tf_op jit(solution)/shard_map/convert_element_type | solution.py:77
  153.9 0.7 convolution_bitcast_fusion.7
  154.9 0.8 fusion.77
  155.7 4.1 %fusion.30 = (bf16[4,256,256]{2,1,0:T(8,128)(2,1)S(1)}, bf16[4,256,256]{2,1,0:T(8,128)(2,1)S(1)}) fusion(bf16[4,256,256]{2,1,0:T(8,128)(2,1)S(1)} %get-tuple-element.12, f32[8,256,512]{2,1,0:T(8,128)S(1)} %fusion.77), kind=kLoop, calls=%fused_computation.63 | loop fusion | flops 2883584 | bytes 5767168 | tf_op jit(solution)/shard_map/convert_element_type | solution.py:50
  159.8 0.8 convolution_bitcast_fusion.6
  161.1 0.8 fusion.84
  161.8 4.7 %fusion.147 = (f32[256,256]{0,1:T(8,128)S(1)}, f32[256,256]{0,1:T(8,128)S(1)}, f32[256,256]{0,1:T(8,128)S(1)}, f32[256,256]{0,1:T(8,128)S(1)}, f32[256,256]{0,1:T(8,128)S(1)}, /*index=5*/f32[256,256]{0,1:T(8,128)S(1)}) fusion(f32[]{:T(128)} %bitcast.11, s32[256]{0:T(256)S(1)} %fusion.169, f32[]{:T(128)} %bitcast.17, f32[]{:T(128)} %bitcast.14), kind=kLoop, calls=%fused_computation.227 | loop fusion | flops 983040 | bytes 1573900 | tf_op jit(solution)/shard_map/mul | solution.py:90
  167.0 0.7 convolution_bitcast_fusion.5
  168.1 0.8 fusion.91
  168.8 4.3 %fusion.26 = (bf16[4,256,256]{2,1,0:T(8,128)(2,1)S(1)}, bf16[4,256,256]{2,1,0:T(8,128)(2,1)S(1)}) fusion(bf16[4,256,256]{2,1,0:T(8,128)(2,1)S(1)} %get-tuple-element.20, f32[8,256,512]{2,1,0:T(8,128)S(1)} %fusion.91), kind=kLoop, calls=%fused_computation.59 | loop fusion | flops 2883584 | bytes 5767168 | tf_op jit(solution)/shard_map/convert_element_type | solution.py:50
  173.2 0.8 convolution_bitcast_fusion.4
  174.3 0.8 fusion.98
  175.6 0.7 convolution_bitcast_fusion.3
  176.6 0.8 fusion.105
  177.4 4.1 %fusion.22 = (bf16[4,256,256]{2,1,0:T(8,128)(2,1)S(1)}, bf16[4,256,256]{2,1,0:T(8,128)(2,1)S(1)}) fusion(bf16[4,256,256]{2,1,0:T(8,128)(2,1)S(1)} %get-tuple-element.28, f32[8,256,512]{2,1,0:T(8,128)S(1)} %fusion.105), kind=kLoop, calls=%fused_computation.55 | loop fusion | flops 2883584 | bytes 5767168 | tf_op jit(solution)/shard_map/convert_element_type | solution.py:50
  181.5 0.8 convolution_bitcast_fusion.2
  182.6 0.8 fusion.112
  183.9 0.7 convolution_bitcast_fusion.1
  184.9 0.8 fusion.119
  185.7 4.4 %fusion.18 = (bf16[4,256,256]{2,1,0:T(8,128)(2,1)S(1)}, bf16[4,256,256]{2,1,0:T(8,128)(2,1)S(1)}) fusion(bf16[4,256,256]{2,1,0:T(8,128)(2,1)S(1)} %get-tuple-element.36, f32[8,256,512]{2,1,0:T(8,128)S(1)} %fusion.119), kind=kLoop, calls=%fused_computation.51 | loop fusion | flops 2883584 | bytes 5767168 | tf_op jit(solution)/shard_map/convert_element_type | solution.py:50
  190.1 0.8 convolution_bitcast_fusion
  191.2 0.8 fusion.126
  192.9 1.2 copy.135
  194.1 6.8 %all-to-all-start = ((bf16[4,16,4096]{2,0,1:T(4,128)(2,1)}), bf16[4,16,4096]{2,0,1:T(4,128)(2,1)S(1)}, u32[]{:S(2)}, u32[]{:S(2)}) async-start(bf16[4,16,4096]{2,0,1:T(4,128)(2,1)} %copy.135), calls=%async_computation | async-start | bytes 1048576 | tf_op jit(solution)/shard_map/all_to_all | solution.py:166
  201.0 14.1 %all-to-all-done = bf16[4,16,4096]{2,0,1:T(4,128)(2,1)S(1)} async-done(((bf16[4,16,4096]{2,0,1:T(4,128)(2,1)}), bf16[4,16,4096]{2,0,1:T(4,128)(2,1)S(1)}, u32[]{:S(2)}, u32[]{:S(2)}) %all-to-all-start) | async-done | bytes 524320 | tf_op jit(solution)/shard_map/all_to_all | solution.py:166
  215.9 1.5 pad_maximum_fusion
  (62 shorter events, 12.1 us)
Async XLA Ops:
  9.5 98.3 %copy-start.1 = (s32[4,2]{0,1:T(2,128)S(1)}, s32[4,2]{0,1:T(2,128)}, u32[]{:S(2)}) copy-start(s32[4,2]{0,1:T(2,128)} %param.15) | copy-start | bytes 100
  106.6 12.8 %copy-start = (f32[3]{0:T(128)S(1)}, f32[3]{0:T(128)}, u32[]{:S(2)}) copy-start(f32[3]{0:T(128)} %param.17) | copy-start | bytes 40
  119.4 29.5 %copy-start.2 = (s32[4,2]{0,1:T(2,128)S(1)}, s32[4,2]{0,1:T(2,128)}, u32[]{:S(2)}) copy-start(s32[4,2]{0,1:T(2,128)} %param.16) | copy-start | bytes 100
  194.1 21.1 %all-to-all-start = ((bf16[4,16,4096]{2,0,1:T(4,128)(2,1)}), bf16[4,16,4096]{2,0,1:T(4,128)(2,1)S(1)}, u32[]{:S(2)}, u32[]{:S(2)}) async-start(bf16[4,16,4096]{2,0,1:T(4,128)(2,1)} %copy.135), calls=%async_computation | async-start | bytes 1048576 | tf_op jit(solution)/shard_map/all_to_all | solution.py:166
where the time goes:
time: 218 us; the launch traced here: 217 us
  blocking collectives  97.1 us (45%)
  local copies, waits for them, and re-layouts  44.5 us (20%)
  other arithmetic  36.9 us (17%)
  matrix products  17.2 us (8%)
  waiting for transfers between devices  14.1 us (6%)
  starting transfers between devices  6.8 us (3%)
    psum x1, blocking collectives, on_device(): lax.psum(partial_field, 'probe').astype(jnp.bfloat16).reshape(SLICES, G, G)  97.1 us
    gather x48, local copies, waits for them, and re-layouts  38.6 us
    convert_element_type x4, other arithmetic, transmit(): (real_part * cosine - imag_part * sine).astype(jnp.bfloat16)  17 us
    all_to_all x1, waiting for transfers between devices, on_device(): lax.all_to_all(pieces, 'probe', split_axis=1, concat_axis=0, tiled=True)  14.1 us
    all_to_all x1, starting transfers between devices, on_device(): lax.all_to_all(pieces, 'probe', split_axis=1, concat_axis=0, tiled=True)  6.8 us
    dot_general x8, matrix products, along_columns(): jnp.einsum('byx,xl->byl', stacked, matrix, preferred_element_type=jnp.flo...  6.17 us
    dot_general x8, matrix products, along_rows(): jnp.einsum('ky,byx->bkx', matrix, stacked, preferred_element_type=jnp.flo...  6.03 us
    convert_element_type x1, other arithmetic, multislice(): (probe_spectrum[0] * cosine + probe_spectrum[1] * sine).astype(jnp.bfloat16)  4.77 us
  transfers between devices with their start and end apart: 1, of which 1 were waited for; matrix products, arithmetic and copies ran while one was open for 0% of the time, Pallas kernels for 0%

commit v1 on v0

v1 whole, which is shorter than its diff:
```python
import math

import jax
import jax.numpy as jnp
import numpy as np
from jax import lax
from jax.experimental import pallas as pl
from jax.experimental.pallas import tpu as pltpu
from jax.sharding import PartitionSpec as P

G = 512
LANES = 128
BF16 = jnp.bfloat16
F32 = jnp.float32


def cosine_fit(scale, odd):
    nodes = 0.125 * (1.0 - np.cos((np.arange(400) + 0.5) * np.pi / 400))
    f = np.sqrt(nodes)
    values = np.sin(np.pi * f) / f if odd else np.cos(np.pi * f)
    fit = np.polynomial.chebyshev.Chebyshev.fit(nodes, values, 4, domain=[0.0, 0.25])
    return [float(scale * c) for c in fit.convert(kind=np.polynomial.Polynomial).coef]


SIN_FIT = cosine_fit(2.0, True)
COS_FIT = cosine_fit(1.0, False)
TURN_HIGH = float(np.float32(np.round(2.0**16 / (2.0 * np.pi)) / 2.0**16))
TURN_LOW = float(1.0 / (2.0 * np.pi) - TURN_HIGH)


def horner(coefficients, g):
    total = coefficients[-1]
    for c in coefficients[-2::-1]:
        total = total * g + c
    return total


def cos_sin_turns(f):
    g = f * f
    twice_sine = f * horner(SIN_FIT, g)
    cosine = horner(COS_FIT, g)
    return (1.0 - 0.5 * (twice_sine * twice_sine), twice_sine * cosine)


def cos_sin(v):
    t = v * TURN_HIGH
    return cos_sin_turns((t - jnp.round(t)) + v * TURN_LOW)


def mirrored(length, tile):
    m = np.arange(length // 2).reshape(-1, tile)
    return np.concatenate([m, length - 1 - m], axis=1).reshape(-1)


def signed(half, tile):
    m = np.arange(half).reshape(-1, tile)
    k = np.concatenate([m, -m], axis=1).reshape(-1)
    second = np.concatenate([np.zeros_like(m), np.ones_like(m)], axis=1).reshape(-1) == 1
    return k, second


class Plan:
    def __init__(self, length):
        n = self.n = length
        kmax = max(k for k in range(n) if 9 * k * k < n * n)
        self.half_y = -(-(kmax + 1) // 8) * 8
        self.rows = 2 * self.half_y
        pix_y = mirrored(n, 8)
        pix_x = mirrored(n, n // 2)
        ky, second_y = signed(self.half_y, 8)
        kx, second_x = signed(n // 2, n // 2)
        scale = 1.0 / math.sqrt(n)

        def forward(freq, pix, odd_slot):
            m = np.where(odd_slot, n - 1 - pix, pix)
            angle = 2.0 * np.pi / n * np.outer(freq, m + 0.5)
            return np.where(odd_slot[None, :], np.sin(angle), np.cos(angle)) * scale

        odd_y = pix_y >= n // 2
        odd_x = pix_x >= n // 2
        self.fwd_y = forward(ky, pix_y, odd_y)
        self.fwd_x = forward(kx, pix_x, odd_x).T

        def inverse(pix, freq, second):
            angle = 2.0 * np.pi / n * np.outer(pix + 0.5, np.abs(freq))
            return np.where(second[None, :], np.sin(angle), np.cos(angle)) * scale

        self.inv_y = inverse(pix_y, ky, second_y)
        self.inv_x = inverse(pix_x, kx, second_x).T
        block = 16
        keep = -(-(kmax + 1) // block) * block
        self.keep = keep
        nat = np.concatenate([np.arange(keep), np.arange(n - keep, n)])
        self.last_y = forward(nat, pix_y, odd_y)
        self.last_x = forward(np.arange(n), pix_x, odd_x).T
        freq = (np.arange(n) + n // 2) % n - n // 2
        q2 = freq[nat][:, None] ** 2 + freq[None, :] ** 2
        self.aperture_last = (9 * q2 < n * n).astype(np.float32)
        q2 = ky[:, None] ** 2 + kx[None, :] ** 2
        self.q2 = q2.astype(np.float32)
        self.aperture = (
            (9 * q2 < n * n) & ~((ky == 0) & second_y)[:, None] & ~((kx == 0) & second_x)[None, :]
        ).astype(np.float32)
        ay = 2.0 * np.pi / n * (np.outer(pix_y, np.arange(n)) % n)
        ax = 2.0 * np.pi / n * (np.outer(np.arange(n), pix_x) % n)
        self.start_y = np.stack(
            [
                np.concatenate([np.cos(ay), -np.sin(ay)], axis=1),
                np.concatenate([np.sin(ay), np.cos(ay)], axis=1),
            ]
        ) * scale
        self.start_x = np.stack(
            [
                np.concatenate([np.cos(ax), -np.sin(ax)], axis=0),
                np.concatenate([np.sin(ax), np.cos(ax)], axis=0),
            ]
        ) * scale
        halves = G // n
        self.grid_y = np.concatenate([pix_y + n * h for h in range(halves)]).astype(np.float32)
        self.grid_x = np.concatenate([pix_x + n * h for h in range(halves)]).astype(np.float32)


def dot(a, b):
    return jnp.dot(a, b, preferred_element_type=F32)


def gather_atoms(block, devices):
    step = 2
    while step < devices:
        pairs = [(i, i ^ step) for i in range(devices)]
        block = jnp.concatenate([block, lax.ppermute(block, "probe", pairs)], axis=0)
        step *= 2
    return block


def build_body(layers, species, amp_ref, width_ref, gy_ref, gx_ref, atoms_ref, out_ref, row_ref, col_ref):
    blocks = atoms_ref.shape[1] // 3
    code = atoms_ref[0, 2 * blocks :, :]
    layer = jnp.floor(code * (1.0 / species))
    kind = code - layer * species
    amp = jnp.zeros_like(code)
    width = jnp.zeros_like(code)
    for k in range(species):
        amp = jnp.where(kind == k, amp_ref[k], amp)
        width = jnp.where(kind == k, width_ref[k], width)
    for b in range(blocks):
        lanes = slice(b * LANES, (b + 1) * LANES)
        w = width[b : b + 1, :]
        a = amp[b : b + 1, :]
        masks = [(layer[b : b + 1, :] == s).astype(F32).astype(BF16) for s in range(layers)]
        y = atoms_ref[0, b : b + 1, :]
        x = atoms_ref[0, blocks + b : blocks + b + 1, :]
        for r in range(0, G, 64):
            rows = slice(r, r + 64)
            d = gy_ref[rows, :] - y
            e = (jnp.exp2(d * d * w) * a).astype(BF16)
            for s in range(layers):
                row_ref[s, rows, lanes] = e * masks[s]
            d = gx_ref[rows, :] - x
            col_ref[rows, lanes] = jnp.exp2(d * d * w).astype(BF16)
    first = pl.program_id(0) == 0
    for s in range(layers):
        part = lax.dot_general(
            row_ref[s], col_ref[...], (((1,), (1,)), ((), ())), preferred_element_type=F32
        )

        @pl.when(first)
        def _():
            out_ref[s] = part

        @pl.when(jnp.logical_not(first))
        def _():
            out_ref[s] += part


def build(plan, atoms, amps, widths, layers):
    segments, height, lanes = atoms.shape
    species = amps.shape[0]
    atom_count = height // 3 * lanes
    grid_y = np.broadcast_to(plan.grid_y[:, None], (G, LANES))
    grid_x = np.broadcast_to(plan.grid_x[:, None], (G, LANES))
    whole = lambda *shape: pl.BlockSpec(shape, lambda i: (0,) * len(shape))
    smem = pl.BlockSpec(memory_space=pltpu.SMEM)

    def body(*refs):
        build_body(layers, species, *refs)

    return pl.pallas_call(
        body,
        out_shape=jax.ShapeDtypeStruct((layers, G, G), F32),
        grid=(segments,),
        in_specs=[
            smem,
            smem,
            whole(G, LANES),
            whole(G, LANES),
            pl.BlockSpec((1, height, lanes), lambda i: (i, 0, 0)),
        ],
        out_specs=whole(layers, G, G),
        scratch_shapes=[pltpu.VMEM((layers, G, atom_count), BF16), pltpu.VMEM((G, atom_count), BF16)],
        name="build",
    )(amps, widths, jnp.asarray(grid_y), jnp.asarray(grid_x), atoms)


def init_body(shift_ref, phase_ref, spec_ref, ty_ref, tx_ref, q2_ref, ap_ref, z_ref, prop_ref, a_ref, b_ref):
    n = spec_ref.shape[-1]
    positions = z_ref.shape[0]
    for layer in range(prop_ref.shape[0]):
        for r in range(0, q2_ref.shape[0], 16):
            rows = slice(r, r + 16)
            c, s = cos_sin(phase_ref[layer] * q2_ref[rows, :])
            prop_ref[layer, 0, rows, :] = ap_ref[rows, :] * c
            prop_ref[layer, 1, rows, :] = -(ap_ref[rows, :] * s)
    for p in range(positions):
        sy = shift_ref[p, 0]
        sx = shift_ref[p, 1]
        for r in range(0, n, 16):
            rows = slice(r, r + 16)
            ky = lax.broadcasted_iota(jnp.int32, (16, n), 0) + r
            kx = lax.broadcasted_iota(jnp.int32, (16, n), 1)
            turns = ((ky * sy + kx * sx) & (n - 1)).astype(F32) * (1.0 / n)
            c, s = cos_sin_turns(turns - jnp.round(turns))
            re = spec_ref[0, rows, :]
            im = spec_ref[1, rows, :]
            a_ref[p, rows, :] = (re * c + im * s).astype(BF16)
            a_ref[p, slice(n + r, n + r + 16), :] = (im * c - re * s).astype(BF16)
        b_ref[p, :, :n] = dot(ty_ref[0], a_ref[p]).astype(BF16)
        b_ref[p, :, n:] = dot(ty_ref[1], a_ref[p]).astype(BF16)
        z_ref[p, 0] = dot(b_ref[p], tx_ref[0])
        z_ref[p, 1] = dot(b_ref[p], tx_ref[1])


def init(plan, shifts, slice_phase, spectrum):
    n = plan.n
    positions = shifts.shape[0]
    vmem = pl.BlockSpec(memory_space=pltpu.VMEM)
    smem = pl.BlockSpec(memory_space=pltpu.SMEM)
    return pl.pallas_call(
        init_body,
        out_shape=(
            jax.ShapeDtypeStruct((positions, 2, n, n), F32),
            jax.ShapeDtypeStruct((slice_phase.shape[0], 2, plan.rows, n), F32),
        ),
        in_specs=[smem, smem, vmem, vmem, vmem, vmem, vmem],
        out_specs=(vmem, vmem),
        scratch_shapes=[pltpu.VMEM((positions, 2 * n, n), BF16), pltpu.VMEM((positions, n, 2 * n), BF16)],
        name="init",
    )(
        shifts,
        slice_phase,
        spectrum,
        jnp.asarray(plan.start_y, BF16),
        jnp.asarray(plan.start_x, BF16),
        jnp.asarray(plan.q2),
        jnp.asarray(plan.aperture),
    )


def halves(x, axis):
    h = x.shape[axis] // 2
    if axis == 0:
        return x[:h], x[h:]
    return x[:, :h], x[:, h:]


def forward_pair(re, im, axis):
    rt, rb = halves(re, axis)
    it, ib = halves(im, axis)
    u = jnp.concatenate([rt + rb, it - ib], axis=axis)
    w = jnp.concatenate([it + ib, rb - rt], axis=axis)
    return u.astype(BF16), w.astype(BF16)


def inverse_pair(re, im, axis):
    rt, rb = halves(re, axis)
    it, ib = halves(im, axis)
    u = jnp.concatenate([rt + rb, ib - it], axis=axis)
    w = jnp.concatenate([it + ib, rt - rb], axis=axis)
    return u.astype(BF16), w.astype(BF16)


def slice_body(plan, direct, off_ref, own_ref, got_ref, z0_ref, prop_ref, fy_ref, fx_ref, iy_ref, ix_ref,
               ly_ref, lx_ref, la_ref, out_ref, v_ref, z_ref, u_ref, y_ref, t_ref, x_ref, sem):
    n = plan.n
    rows_f = plan.rows
    positions = z0_ref.shape[0]
    layers = own_ref.shape[0]
    fetch = pltpu.make_async_copy(z0_ref, z_ref, sem)
    fetch.start()

    def combine(layer):
        for r in range(0, G, 16):
            rows = slice(r, r + 16)
            total = own_ref[layer, rows, :] + got_ref[layer, rows, :].astype(F32)
            v_ref[rows, :] = total.astype(BF16).astype(F32)

    lane = lax.broadcasted_iota(jnp.int32, (16, n), 1)
    pixel_x = jnp.where(lane < n // 2, lane, n + n // 2 - 1 - lane)
    sub = lax.broadcasted_iota(jnp.int32, (16, n), 0)

    def transmit(p):
        oy = off_ref[p, 0]
        ox = off_ref[p, 1]
        inside_x = pixel_x >= ox
        for g in range(n // 16):
            rows = slice(16 * g, 16 * g + 16)
            far = slice(n + 16 * g, n + 16 * g + 16)
            pixel_y = jnp.where(sub < 8, sub + 8 * g, n + 7 - 8 * g - sub)
            near_v = jnp.where(inside_x, v_ref[rows, :n], v_ref[rows, n:])
            far_v = jnp.where(inside_x, v_ref[far, :n], v_ref[far, n:])
            c, s = cos_sin(jnp.where(pixel_y >= oy, near_v, far_v))
            zr = z_ref[p, 0, rows, :]
            zi = z_ref[p, 1, rows, :]
            u, w = forward_pair(zr * c - zi * s, zr * s + zi * c, 0)
            u_ref[p, 0, rows, :] = u
            u_ref[p, 1, rows, :] = w

    def step(layer, carry):
        combine(layer)
        for p in range(positions):
            transmit(p)
            y_ref[p, 0, :rows_f] = dot(fy_ref[...], u_ref[p, 0])
            y_ref[p, 1, :rows_f] = dot(fy_ref[...], u_ref[p, 1])
            for g in range(rows_f // 16):
                rows = slice(16 * g, 16 * g + 16)
                low = slice(rows_f + 16 * g, rows_f + 16 * g + 16)
                t_ref[p, rows, :], t_ref[p, low, :] = forward_pair(y_ref[p, 0, rows, :], y_ref[p, 1, rows, :], 1)
            x_ref[p, : 2 * rows_f] = dot(t_ref[p, : 2 * rows_f], fx_ref[...])
            for g in range(rows_f // 16):
                rows = slice(16 * g, 16 * g + 16)
                low = slice(rows_f + 16 * g, rows_f + 16 * g + 16)
                re = x_ref[p, rows, :]
                im = x_ref[p, low, :]
                pr = prop_ref[layer, 0, rows, :]
                pi = prop_ref[layer, 1, rows, :]
                t_ref[p, rows, :], t_ref[p, low, :] = inverse_pair(re * pr - im * pi, re * pi + im * pr, 1)
            x_ref[p, : 2 * rows_f] = dot(t_ref[p, : 2 * rows_f], ix_ref[...])
            for g in range(rows_f // 16):
                rows = slice(16 * g, 16 * g + 16)
                low = slice(rows_f + 16 * g, rows_f + 16 * g + 16)
                t_ref[p, rows, :], t_ref[p, low, :] = inverse_pair(x_ref[p, rows, :], x_ref[p, low, :], 0)
            z_ref[p, 0] = dot(iy_ref[...], t_ref[p, :rows_f])
            z_ref[p, 1] = dot(iy_ref[...], t_ref[p, rows_f : 2 * rows_f])
        return carry

    fetch.wait()
    lax.fori_loop(0, layers - 1, step, 0)
    combine(layers - 1)
    keep = plan.keep
    for p in range(positions):
        transmit(p)
        y_ref[p, 0] = dot(ly_ref[...], u_ref[p, 0])
        y_ref[p, 1] = dot(ly_ref[...], u_ref[p, 1])
        count = 2 * keep
        for g in range(count // 16):
            rows = slice(16 * g, 16 * g + 16)
            low = slice(count + 16 * g, count + 16 * g + 16)
            t_ref[p, rows, :], t_ref[p, low, :] = forward_pair(y_ref[p, 0, rows, :], y_ref[p, 1, rows, :], 1)
        x_ref[p] = dot(t_ref[p], lx_ref[...])
        for g in range(n // 16):
            r = 16 * g
            if r < keep:
                src = r
            elif r >= n - keep:
                src = r - (n - 2 * keep)
            else:
                src = None
            if src is None:
                value = jnp.zeros((16, n), BF16)
            else:
                re = x_ref[p, slice(src, src + 16), :]
                im = x_ref[p, slice(count + src, count + src + 16), :]
                value = (la_ref[slice(src, src + 16), :] * (re * re + im * im)).astype(BF16)
            if direct:
                out_ref[g, p] = value
            else:
                out_ref[p, slice(r, r + 16), :] = value


def multislice(plan, offsets, own, got, start, prop, direct):
    n = plan.n
    positions = start.shape[0]
    vmem = pl.BlockSpec(memory_space=pltpu.VMEM)
    smem = pl.BlockSpec(memory_space=pltpu.SMEM)
    shape = (n // 16, positions, 16, n) if direct else (positions, n, n)
    count = 2 * plan.keep

    def body(*refs):
        slice_body(plan, direct, *refs)

    return pl.pallas_call(
        body,
        out_shape=jax.ShapeDtypeStruct(shape, BF16),
        in_specs=[smem, vmem, vmem, pl.BlockSpec(memory_space=pl.ANY)] + [vmem] * 8,
        out_specs=vmem,
        scratch_shapes=[
            pltpu.VMEM((G, G), F32),
            pltpu.VMEM((positions, 2, n, n), F32),
            pltpu.VMEM((positions, 2, n, n), BF16),
            pltpu.VMEM((positions, 2, count, n), F32),
            pltpu.VMEM((positions, 2 * count, n), BF16),
            pltpu.VMEM((positions, 2 * count, n), F32),
            pltpu.SemaphoreType.DMA,
        ],
        name="multislice",
    )(
        offsets,
        own,
        got,
        start,
        prop,
        jnp.asarray(plan.fwd_y, BF16),
        jnp.asarray(plan.fwd_x, BF16),
        jnp.asarray(plan.inv_y, BF16),
        jnp.asarray(plan.inv_x, BF16),
        jnp.asarray(plan.last_y, BF16),
        jnp.asarray(plan.last_x, BF16),
        jnp.asarray(plan.aperture_last),
    )


def scan_matrix(positions):
    index = np.arange(positions)
    angle = 2.0 * np.pi / positions * (np.outer(index, index) % positions)
    return np.concatenate([np.cos(angle), -np.sin(angle)]) / math.sqrt(positions)


def on_device(
    atom_positions,
    atom_species,
    atom_slice,
    species_amp,
    species_width,
    probe_spectrum,
    window_offsets,
    probe_shifts,
    slice_phase,
):
    devices = lax.axis_size("probe")
    n = probe_spectrum.shape[-1]
    layers = slice_phase.shape[0] + 1
    plan = Plan(n)
    species = species_amp.shape[0]
    atom_rows = atom_species.shape[0] // LANES
    code = (atom_slice * species + atom_species).astype(F32).reshape(atom_rows, LANES)
    atoms = jnp.concatenate([atom_positions.reshape(2 * atom_rows, LANES), code], axis=0)[None]
    widths = -0.5 * math.log2(math.e) / (species_width * species_width)
    atoms = gather_atoms(atoms, devices)
    own = build(plan, atoms, species_amp, widths, layers)
    pairs = [(i, i ^ 1) for i in range(devices)]
    got = lax.ppermute(own.astype(BF16), "probe", pairs)
    shifts = (probe_shifts + window_offsets) & (n - 1)
    start, prop = init(plan, shifts, slice_phase, probe_spectrum)
    rows = n // devices
    direct = rows % 16 == 0
    intensity = multislice(plan, window_offsets, own, got, start, prop, direct)
    positions = window_offsets.shape[0]
    if direct:
        received = lax.all_to_all(intensity, "probe", split_axis=0, concat_axis=0, tiled=True)
    else:
        pieces = intensity.reshape(positions, devices, rows, n)
        received = lax.all_to_all(pieces, "probe", split_axis=1, concat_axis=0, tiled=True)
    count = positions * devices
    received = received.reshape(count, rows * n)
    product = dot(jnp.asarray(scan_matrix(count), BF16), received)
    return product.reshape(2, count, rows * n)


def solution(mesh):
    placed = (
        P(None, ("groups", "probe")),
        P(("groups", "probe")),
        P(("groups", "probe")),
        P(),
        P(),
        P(),
        P(("groups", "probe"), None),
        P(("groups", "probe"), None),
        P(),
    )
    return jax.shard_map(
        on_device, mesh=mesh, in_specs=placed, out_specs=P(None, "groups", "probe"), check_vma=False
    )
```

time: 218 us -> 114 us (0.52)
  blocking collectives: 97.1 us -> 21.1 us
  Pallas kernels: 0 us -> 65.8 us
  local copies, waits for them, and re-layouts: 44.5 us -> 5.42 us
  other arithmetic: 36.9 us -> 6.9 us
  matrix products: 17.2 us -> 1.73 us
  waiting for transfers between devices: 14.1 us -> 4.4 us
    psum x1 -> x0, blocking collectives: 97.1 us -> none  [on_device(): lax.psum(partial_field, 'probe').astype(jnp.bfloat16).reshape(SLICES, G, G)]
    pallas_call x0 -> x3, Pallas kernels: none -> 65.8 us  [the longest x1 41.4 us: build(): pl.pallas_call(body, out_shape=jax.ShapeDtypeStruct((layers, G, G), F32),...]
    gather x48 -> x0, local copies, waits for them, and re-layouts: 38.6 us -> none
    convert_element_type x21 -> x1, other arithmetic: 28.5 us -> 3.8 us  [on_device(): got = lax.ppermute(own.astype(BF16), 'probe', pairs)]
    all_to_all x0 -> x1, blocking collectives: none -> 21.1 us  [on_device(): lax.all_to_all(intensity, 'probe', split_axis=0, concat_axis=0, tiled=True)]
    dot_general x18 -> x1, matrix products: 17.2 us -> 1.73 us  [dot(): return jnp.dot(a, b, preferred_element_type=F32)]
    all_to_all x1 -> x0, waiting for transfers between devices: 14.1 us -> none  [on_device(): lax.all_to_all(pieces, 'probe', split_axis=1, concat_axis=0, tiled=True)]
    ppermute x0 -> x4, starting transfers between devices: none -> 8.11 us  [the longest x3 8.11 us: gather_atoms(): lax.ppermute(block, 'probe', pairs)]
  transfers between devices with their start and end apart: 1 -> 4, of which waited for: 1 -> 3; matrix products, arithmetic and copies ran while one was open for 0% -> 2% of each run, Pallas kernels for 0% -> 5%
where the time goes in v1:
time: 114 us; the launch traced here: 113 us
  Pallas kernels  65.8 us (58%)
  blocking collectives  21.1 us (19%)
  starting transfers between devices  8.11 us (7%)
  other arithmetic  6.9 us (6%)
  local copies, waits for them, and re-layouts  5.42 us (5%)
  waiting for transfers between devices  4.4 us (4%)
  matrix products  1.73 us (2%)
    pallas_call x1, Pallas kernels, build(): pl.pallas_call(body, out_shape=jax.ShapeDtypeStruct((layers, G, G), F32),...  41.4 us
    all_to_all x1, blocking collectives, on_device(): lax.all_to_all(intensity, 'probe', split_axis=0, concat_axis=0, tiled=True)  21.1 us
    pallas_call x1, Pallas kernels, multislice(): pl.pallas_call(body, out_shape=jax.ShapeDtypeStruct(shape, BF16), in_spec...  18.8 us
    ppermute x3, starting transfers between devices, gather_atoms(): lax.ppermute(block, 'probe', pairs)  8.11 us
    pallas_call x1, Pallas kernels, init(): pl.pallas_call(init_body, out_shape=(jax.ShapeDtypeStruct((positions, 2,...  5.6 us
    ppermute x3, waiting for transfers between devices, gather_atoms(): lax.ppermute(block, 'probe', pairs)  4.4 us
    convert_element_type x1, other arithmetic, on_device(): got = lax.ppermute(own.astype(BF16), 'probe', pairs)  3.8 us
    another operation x2, local copies, waits for them, and re-layouts  3.03 us
  transfers between devices with their start and end apart: 4, of which 3 were waited for; matrix products, arithmetic and copies ran while one was open for 2% of the time, Pallas kernels for 5%

profile of v1, /device:TPU:0, one launch (start us, length us, event | category | flops | bytes accessed | tf_op | source)
XLA Modules:
  0.0 113.5 jit_solution(6398017208474298409)
XLA Ops:
  0.0 0.7 reshape.12
  0.7 0.7 convert_bitcast_fusion
  1.4 3.0 %collective-permute-start = (f32[1,24,128]{2,1,0:T(8,128)S(1)}, f32[1,24,128]{2,1,0:T(8,128)S(1)}, u32[]{:S(2)}, u32[]{:S(2)}) collective-permute-start(f32[1,24,128]{2,1,0:T(8,128)S(1)} %maximum_bitcast_fusion), channel_id=1, source_target_pairs={{0,2},{1,3},{2,0},{3,1},{4,6},{5,7},{6,4},{7,5},{8,10},{9,11},{10,... | collective-permute-start | bytes 36872 | tf_op jit(solution)/shard_map/ppermute | solution.py:131
  4.4 1.7 %collective-permute-done = f32[1,24,128]{2,1,0:T(8,128)S(1)} collective-permute-done((f32[1,24,128]{2,1,0:T(8,128)S(1)}, f32[1,24,128]{2,1,0:T(8,128)S(1)}, u32[]{:S(2)}, u32[]{:S(2)}) %collective-permute-start) | collective-permute-done | bytes 12320 | tf_op jit(solution)/shard_map/ppermute | solution.py:131
  6.1 2.1 %collective-permute-start.1 = (f32[2,24,128]{2,1,0:T(8,128)S(1)}, f32[2,24,128]{2,1,0:T(8,128)S(1)}, u32[]{:S(2)}, u32[]{:S(2)}) collective-permute-start(f32[2,24,128]{2,1,0:T(8,128)S(1)} %pad_maximum_fusion.2), channel_id=1, source_target_pairs={{0,4},{1,5},{2,6},{3,7},{4,0},{5,1},{6,2},{7,3},{8,12},{9,13},{10,... | collective-permute-start | bytes 73736 | tf_op jit(solution)/shard_map/ppermute | solution.py:131
  8.2 1.8 %collective-permute-done.1 = f32[2,24,128]{2,1,0:T(8,128)S(1)} collective-permute-done((f32[2,24,128]{2,1,0:T(8,128)S(1)}, f32[2,24,128]{2,1,0:T(8,128)S(1)}, u32[]{:S(2)}, u32[]{:S(2)}) %collective-permute-start.1) | collective-permute-done | bytes 24608 | tf_op jit(solution)/shard_map/ppermute | solution.py:131
  10.0 3.0 %collective-permute-start.2 = (f32[4,24,128]{2,1,0:T(8,128)S(1)}, f32[4,24,128]{2,1,0:T(8,128)S(1)}, u32[]{:S(2)}, u32[]{:S(2)}) collective-permute-start(f32[4,24,128]{2,1,0:T(8,128)S(1)} %pad_maximum_fusion.1), channel_id=1, source_target_pairs={{0,8},{1,9},{2,10},{3,11},{4,12},{5,13},{6,14},{7,15},{8,0},{9,1},... | collective-permute-start | bytes 147464 | tf_op jit(solution)/shard_map/ppermute | solution.py:131
  13.0 1.1 %multiply_divide_fusion.refs_1_ = f32[8]{0:T(128)} fusion(f32[8]{0:T(128)} %param.27), kind=kLoop, calls=%fused_computation.6 | loop fusion | flops 16 | bytes 64 | tf_op jit(solution)/shard_map/div | solution.py:447
  14.2 0.9 collective-permute-done.2
  15.1 0.6 pad_maximum_fusion.refs_4_
  15.7 1.5 %jit_solution_.6.refs_2_ = f32[512,128]{1,0:T(8,128)} broadcast(f32[512]{0:T(512)} %constant.34.clone), dimensions={0} | broadcast | bytes 264192 | tf_op jit(solution)
  17.2 1.5 %jit_solution_.7.refs_3_ = f32[512,128]{1,0:T(8,128)} broadcast(f32[512]{0:T(512)} %constant.35.clone), dimensions={0} | broadcast | bytes 264192 | tf_op jit(solution)
  18.8 41.4 %build.1.refs_1_ = f32[4,512,512]{2,1,0:T(8,128)} custom-call(f32[8]{0:T(128)} %refs_0_.2, f32[8]{0:T(128)} %multiply_divide_fusion.refs_1_, f32[512,128]{1,0:T(8,128)} %jit_solution_.6.refs_2_, f32[512,128]{1,0:T(8,128)} %jit_solution_.7.refs_3_, f32[8,24,128]{2,1,0:T(8,128)} %pad_maximum_fusion.refs_4_), custom_call_target="tpu_custom_call" | custom-call | tf_op jit(solution)/shard_map/build/pallas_call | solution.py:188
  60.1 0.0 copy-start.3
  60.1 0.0 copy-start.4
  60.1 3.8 %convert_element_type.7 = bf16[4,512,512]{2,1,0:T(8,128)(2,1)} convert(f32[4,512,512]{2,1,0:T(8,128)} %build.1.refs_1_) | non-fusion elementwise | flops 1048576 | bytes 6291456 | tf_op jit(solution)/shard_map/convert_element_type | solution.py:451
  63.9 0.0 collective-permute-start.3
  63.9 0.0 copy-done.3
  63.9 0.1 copy.26.refs_0_
  64.0 0.0 copy-done.4
  64.0 0.0 copy-start.2
  64.0 0.1 copy.24
  64.1 0.6 add_and_fusion.shift_ref
  64.7 5.6 %init.1 = (f32[4,2,256,256]{3,2,1,0:T(8,128)}, f32[3,2,176,256]{3,2,1,0:T(8,128)}) custom-call(s32[4,2]{1,0:T(4,128)} %add_and_fusion.shift_ref, f32[3]{0:T(128)} %phase_ref.1, f32[2,256,256]{2,1,0:T(8,128)} %spec_ref.1, bf16[2,256,512]{2,1,0:T(8,128)(2,1)} %constant.36.clone.ty_ref, bf16[2,512,256]{2,1,0:T(8,128)(2,1)} %constant.37.clone.tx_ref, ...), custom_call_target="tpu_custom_call" | custom-call | tf_op jit(solution)/shard_map/init/pallas_call | solution.py:238
  70.3 0.0 collective-permute-done.3.refs_2_
  70.3 0.0 copy-start
  70.3 0.0 copy-done.2
  70.3 1.3 %copy-done = bf16[4,512,512]{2,1,0:T(8,128)(2,1)} copy-done((bf16[4,512,512]{2,1,0:T(8,128)(2,1)}, bf16[4,512,512]{2,1,0:T(8,128)(2,1)S(1)}, u32[]{:S(2)}) %copy-start) | copy-done | bytes 2097176
  71.6 18.8 %multislice.1 = bf16[16,4,16,256]{3,2,1,0:T(8,128)(2,1)} custom-call(s32[4,2]{1,0:T(4,128)} %copy-done.2, f32[4,512,512]{2,1,0:T(8,128)} %build.1.refs_1_, bf16[4,512,512]{2,1,0:T(8,128)(2,1)} %copy-done, f32[4,2,256,256]{3,2,1,0:T(8,128)} %get-tuple-element.7.refs_3_, f32[3,2,176,256]{3,2,1,0:T(8,128)} %get-tuple-element.8.refs_4_, ...), custom_call_target="tpu_custom_call" | custom-call | tf_op jit(solution)/shard_map/multislice/pallas_call | solution.py:391
  90.4 0.0 copy-start.1
  90.5 21.1 %all_to_all.5 = bf16[16,4,16,256]{3,2,1,0:T(8,128)(2,1)S(1)} all-to-all(bf16[16,4,16,256]{3,2,1,0:T(8,128)(2,1)} %multislice.1), channel_id=1, replica_groups=mesh['groups'=2,'probe'=16] {'probe'}, dimensions={0} | all-to-all | bytes 1048576 | tf_op jit(solution)/shard_map/all_to_all | solution.py:459
  111.5 0.2 copy.27
  111.7 0.0 copy-done.1
  111.7 1.7 %fusion = f32[128,4096]{1,0:T(8,128)} fusion(bf16[128,64]{1,0:T(8,128)(2,1)S(1)} %copy-done.1, bf16[64,4096]{1,0:T(8,128)(2,1)S(1)} %bitcast.11), kind=kOutput, calls=%fused_computation.7 | convolution fusion | flops 67108864 | bytes 2637824 | tf_op jit(solution)/shard_map/dot_general | solution.py:124
  (3 shorter events, 0.0 us)
Async XLA Ops:
  1.4 4.7 %collective-permute-start = (f32[1,24,128]{2,1,0:T(8,128)S(1)}, f32[1,24,128]{2,1,0:T(8,128)S(1)}, u32[]{:S(2)}, u32[]{:S(2)}) collective-permute-start(f32[1,24,128]{2,1,0:T(8,128)S(1)} %maximum_bitcast_fusion), channel_id=1, source_target_pairs={{0,2},{1,3},{2,0},{3,1},{4,6},{5,7},{6,4},{7,5},{8,10},{9,11},{10,... | collective-permute-start | bytes 36872 | tf_op jit(solution)/shard_map/ppermute | solution.py:131
  6.1 3.9 %collective-permute-start.1 = (f32[2,24,128]{2,1,0:T(8,128)S(1)}, f32[2,24,128]{2,1,0:T(8,128)S(1)}, u32[]{:S(2)}, u32[]{:S(2)}) collective-permute-start(f32[2,24,128]{2,1,0:T(8,128)S(1)} %pad_maximum_fusion.2), channel_id=1, source_target_pairs={{0,4},{1,5},{2,6},{3,7},{4,0},{5,1},{6,2},{7,3},{8,12},{9,13},{10,... | collective-permute-start | bytes 73736 | tf_op jit(solution)/shard_map/ppermute | solution.py:131
  10.0 5.1 %collective-permute-start.2 = (f32[4,24,128]{2,1,0:T(8,128)S(1)}, f32[4,24,128]{2,1,0:T(8,128)S(1)}, u32[]{:S(2)}, u32[]{:S(2)}) collective-permute-start(f32[4,24,128]{2,1,0:T(8,128)S(1)} %pad_maximum_fusion.1), channel_id=1, source_target_pairs={{0,8},{1,9},{2,10},{3,11},{4,12},{5,13},{6,14},{7,15},{8,0},{9,1},... | collective-permute-start | bytes 147464 | tf_op jit(solution)/shard_map/ppermute | solution.py:131
  60.1 3.8 %copy-start.3 = (s32[4,2]{0,1:T(2,128)S(1)}, s32[4,2]{0,1:T(2,128)}, u32[]{:S(2)}) copy-start(s32[4,2]{0,1:T(2,128)} %param.29) | copy-start | bytes 100
  60.1 3.9 %copy-start.4 = (s32[4,2]{0,1:T(2,128)S(1)}, s32[4,2]{0,1:T(2,128)}, u32[]{:S(2)}) copy-start(s32[4,2]{0,1:T(2,128)} %param.30) | copy-start | bytes 100
  63.9 6.4 %collective-permute-start.3 = (bf16[4,512,512]{2,1,0:T(8,128)(2,1)}, bf16[4,512,512]{2,1,0:T(8,128)(2,1)S(1)}, u32[]{:S(2)}, u32[]{:S(2)}) collective-permute-start(bf16[4,512,512]{2,1,0:T(8,128)(2,1)} %convert_element_type.7), channel_id=1, source_target_pairs={{0,1},{1,0},{2,3},{3,2},{4,5},{5,4},{6,7},{7,6},{8,9},{9,8},{10,11... | collective-permute-start | bytes 6291464 | tf_op jit(solution)/shard_map/ppermute | solution.py:451
  64.0 6.3 %copy-start.2 = (s32[4,2]{1,0:T(4,128)}, s32[4,2]{1,0:T(4,128)S(1)}, u32[]{:S(2)}) copy-start(s32[4,2]{1,0:T(4,128)S(1)} %copy.26.refs_0_) | copy-start | bytes 100
  70.3 1.3 %copy-start = (bf16[4,512,512]{2,1,0:T(8,128)(2,1)}, bf16[4,512,512]{2,1,0:T(8,128)(2,1)S(1)}, u32[]{:S(2)}) copy-start(bf16[4,512,512]{2,1,0:T(8,128)(2,1)S(1)} %collective-permute-done.3.refs_2_) | copy-start | bytes 6291460
  90.4 21.3 %copy-start.1 = (bf16[128,64]{1,0:T(8,128)(2,1)S(1)}, bf16[128,64]{1,0:T(8,128)(2,1)}, u32[]{:S(2)}) copy-start(bf16[128,64]{1,0:T(8,128)(2,1)} %constant.47.clone) | copy-start | bytes 49156

commit v2 on v1

--- a/solution.py
+++ b/solution.py
@@ -14,16 +14,14 @@
 F32 = jnp.float32
 
 
-def cosine_fit(scale, odd):
+def sine_fit():
     nodes = 0.125 * (1.0 - np.cos((np.arange(400) + 0.5) * np.pi / 400))
     f = np.sqrt(nodes)
-    values = np.sin(np.pi * f) / f if odd else np.cos(np.pi * f)
-    fit = np.polynomial.chebyshev.Chebyshev.fit(nodes, values, 4, domain=[0.0, 0.25])
-    return [float(scale * c) for c in fit.convert(kind=np.polynomial.Polynomial).coef]
-
-
-SIN_FIT = cosine_fit(2.0, True)
-COS_FIT = cosine_fit(1.0, False)
+    fit = np.polynomial.chebyshev.Chebyshev.fit(nodes, np.sin(np.pi * f) / f, 4, domain=[0.0, 0.25])
+    return [float(c) for c in fit.convert(kind=np.polynomial.Polynomial).coef]
+
+
+SIN_FIT = sine_fit()
 TURN_HIGH = float(np.float32(np.round(2.0**16 / (2.0 * np.pi)) / 2.0**16))
 TURN_LOW = float(1.0 / (2.0 * np.pi) - TURN_HIGH)
 
@@ -36,10 +34,10 @@
 
 
 def cos_sin_turns(f):
-    g = f * f
-    twice_sine = f * horner(SIN_FIT, g)
-    cosine = horner(COS_FIT, g)
-    return (1.0 - 0.5 * (twice_sine * twice_sine), twice_sine * cosine)
+    sine = f * horner(SIN_FIT, f * f)
+    square = sine * sine
+    cosine_square = jnp.maximum(1.0 - square, 1e-30)
+    return (1.0 - 2.0 * square, 2.0 * sine * (cosine_square * lax.rsqrt(cosine_square)))
 
 
 def cos_sin(v):
@@ -115,9 +113,6 @@
                 np.concatenate([np.sin(ax), np.cos(ax)], axis=0),
             ]
         ) * scale
-        halves = G // n
-        self.grid_y = np.concatenate([pix_y + n * h for h in range(halves)]).astype(np.float32)
-        self.grid_x = np.concatenate([pix_x + n * h for h in range(halves)]).astype(np.float32)
 
 
 def dot(a, b):
@@ -125,92 +120,250 @@
 
 
 def gather_atoms(block, devices):
+    steps = []
     step = 2
     while step < devices:
-        pairs = [(i, i ^ step) for i in range(devices)]
-        block = jnp.concatenate([block, lax.ppermute(block, "probe", pairs)], axis=0)
+        steps.append(step)
         step *= 2
-    return block
-
-
-def build_body(layers, species, amp_ref, width_ref, gy_ref, gx_ref, atoms_ref, out_ref, row_ref, col_ref):
-    blocks = atoms_ref.shape[1] // 3
-    code = atoms_ref[0, 2 * blocks :, :]
-    layer = jnp.floor(code * (1.0 / species))
-    kind = code - layer * species
-    amp = jnp.zeros_like(code)
-    width = jnp.zeros_like(code)
-    for k in range(species):
-        amp = jnp.where(kind == k, amp_ref[k], amp)
-        width = jnp.where(kind == k, width_ref[k], width)
-    for b in range(blocks):
-        lanes = slice(b * LANES, (b + 1) * LANES)
-        w = width[b : b + 1, :]
-        a = amp[b : b + 1, :]
-        masks = [(layer[b : b + 1, :] == s).astype(F32).astype(BF16) for s in range(layers)]
-        y = atoms_ref[0, b : b + 1, :]
-        x = atoms_ref[0, blocks + b : blocks + b + 1, :]
-        for r in range(0, G, 64):
-            rows = slice(r, r + 64)
-            d = gy_ref[rows, :] - y
-            e = (jnp.exp2(d * d * w) * a).astype(BF16)
-            for s in range(layers):
-                row_ref[s, rows, lanes] = e * masks[s]
-            d = gx_ref[rows, :] - x
-            col_ref[rows, lanes] = jnp.exp2(d * d * w).astype(BF16)
-    first = pl.program_id(0) == 0
+    for step in steps[:-1]:
+        block = jnp.concatenate([block, swap(block, step, devices)], axis=0)
+    if not steps:
+        return [block]
+    return [block, swap(block, steps[-1], devices)]
+
+
+def swap(block, step, devices):
+    return lax.ppermute(block, "probe", [(i, i ^ step) for i in range(devices)])
+
+
+def sort_body(layers, species, pos_ref, kind_ref, layer_ref, kind_row_ref, layer_row_ref, out_ref, one_ref):
+    rows = layer_ref.shape[0]
+    count = rows * LANES
+    owned = [(layer_ref[...] == s).astype(F32) for s in range(layers)]
+    onehot = jnp.concatenate(owned, axis=0).astype(BF16)
+    i = lax.broadcasted_iota(jnp.int32, (LANES, LANES), 0)
+    j = lax.broadcasted_iota(jnp.int32, (LANES, LANES), 1)
+    rank = dot(onehot, (i < j).astype(F32).astype(BF16))
+    total = dot(onehot, jnp.ones((LANES, LANES), BF16)).astype(BF16)
+    height = layers * rows
+    i = lax.broadcasted_iota(jnp.int32, (height, height), 0)
+    j = lax.broadcasted_iota(jnp.int32, (height, height), 1)
+    rank = rank + dot((j < i).astype(F32).astype(BF16), total)
+    place = jnp.zeros((rows, LANES), F32)
     for s in range(layers):
-        part = lax.dot_general(
-            row_ref[s], col_ref[...], (((1,), (1,)), ((), ())), preferred_element_type=F32
-        )
-
-        @pl.when(first)
-        def _():
-            out_ref[s] = part
-
-        @pl.when(jnp.logical_not(first))
-        def _():
-            out_ref[s] += part
-
-
-def build(plan, atoms, amps, widths, layers):
-    segments, height, lanes = atoms.shape
-    species = amps.shape[0]
-    atom_count = height // 3 * lanes
-    grid_y = np.broadcast_to(plan.grid_y[:, None], (G, LANES))
-    grid_x = np.broadcast_to(plan.grid_x[:, None], (G, LANES))
-    whole = lambda *shape: pl.BlockSpec(shape, lambda i: (0,) * len(shape))
-    smem = pl.BlockSpec(memory_space=pltpu.SMEM)
+        place = place + owned[s] * rank[s * rows : (s + 1) * rows, :]
+    place = place.astype(jnp.int32)
+    sub = lax.broadcasted_iota(jnp.int32, (16, 2 * LANES), 0)
+    for b in range(0, rows, 2):
+        wanted = jnp.concatenate([place[b : b + 1, :], place[b + 1 : b + 2, :]], axis=1)
+        for r in range(0, count, 16):
+            hit = (sub + r == wanted).astype(F32).astype(BF16)
+            one_ref[slice(r, r + 16), slice(b * LANES, (b + 2) * LANES)] = hit
+    code = (kind_row_ref[...] + species * layer_row_ref[...]).astype(F32)
+    values = jnp.concatenate([pos_ref[...], code], axis=0)
+    high = values.astype(BF16)
+    rest = values - high.astype(F32)
+    middle = rest.astype(BF16)
+    low = (rest - middle.astype(F32)).astype(BF16)
+    parts = [
+        lax.dot_general(p, one_ref[...], (((1,), (1,)), ((), ())), preferred_element_type=F32)
+        for p in (high, middle, low)
+    ]
+    out_ref[0] = (parts[0] + parts[1]) + parts[2]
+
+
+def sort_atoms(positions, kind, layer, layers, species):
+    count = kind.shape[0]
+    rows = count // LANES
 
     def body(*refs):
-        build_body(layers, species, *refs)
+        sort_body(layers, species, *refs)
 
     return pl.pallas_call(
         body,
-        out_shape=jax.ShapeDtypeStruct((layers, G, G), F32),
-        grid=(segments,),
-        in_specs=[
-            smem,
-            smem,
-            whole(G, LANES),
-            whole(G, LANES),
-            pl.BlockSpec((1, height, lanes), lambda i: (i, 0, 0)),
-        ],
-        out_specs=whole(layers, G, G),
-        scratch_shapes=[pltpu.VMEM((layers, G, atom_count), BF16), pltpu.VMEM((G, atom_count), BF16)],
+        out_shape=jax.ShapeDtypeStruct((1, 3, count), F32),
+        scratch_shapes=[pltpu.VMEM((count, count), BF16)],
+        name="sort",
+    )(
+        positions,
+        kind.reshape(rows, LANES),
+        layer.reshape(rows, LANES),
+        kind.reshape(1, count),
+        layer.reshape(1, count),
+    )
+
+
+def build_body(layers, species, n, amp_ref, width_ref, *refs):
+    *atom_refs, out_ref, gy_ref, gx_ref, acc_ref, all_ref, bound_ref, row_a, col_a, lay_a, row_b, col_b, lay_b = refs
+    count = all_ref.shape[-1]
+    chunks = count // LANES
+    window = min(4, chunks)
+    sub = lax.broadcasted_iota(jnp.int32, (16, LANES), 0)
+    for h in range(G // n):
+        for r in range(0, n, 16):
+            rows = slice(h * n + r, h * n + r + 16)
+            pixel = jnp.where(sub < 8, sub + r // 2, n + 7 - r // 2 - sub) + h * n
+            gy_ref[rows, :] = pixel.astype(F32)
+            pixel = jnp.where(sub + r < n // 2, sub + r, n + n // 2 - 1 - r - sub) + h * n
+            gx_ref[rows, :] = pixel.astype(F32)
+    filled = 0
+    for ref in atom_refs:
+        all_ref[filled : filled + ref.shape[0]] = ref[...]
+        filled += ref.shape[0]
+
+    segments = filled
+
+    def find_bounds(segment, carry):
+        layer = jnp.floor(all_ref[segment, 2:3, :] * (1.0 / species))
+        bound_ref[segment, 0] = 0
+        for s in range(1, layers):
+            bound_ref[segment, s] = jnp.sum((layer < s).astype(F32)).astype(jnp.int32)
+        bound_ref[segment, layers] = count
+        return carry
+
+    lax.fori_loop(0, segments, find_bounds, 0, unroll=min(segments, 8))
+
+    def factors(segment, b, row_ref, col_ref, lay_ref):
+        static = isinstance(b, int)
+        lanes = slice(b * LANES, (b + 1) * LANES) if static else pl.ds(pl.multiple_of(b * LANES, LANES), LANES)
+        code = all_ref[segment, 2:3, lanes]
+        layer = jnp.floor(code * (1.0 / species))
+        kind = code - layer * species
+        a = jnp.zeros_like(code)
+        w = jnp.ones_like(code)
+        for k in range(species):
+            a = jnp.where(kind == k, amp_ref[k], a)
+            w = jnp.where(kind == k, width_ref[k], w)
+        w = (-0.5 * math.log2(math.e)) / (w * w)
+        lay_ref[b] = layer
+        y = all_ref[segment, 0:1, lanes]
+        x = all_ref[segment, 1:2, lanes]
+        for r in range(0, G, 16):
+            rows = slice(r, r + 16)
+            d = gy_ref[rows, :] - y
+            row_ref[b, rows, :] = (jnp.exp2(d * d * w) * a).astype(BF16)
+            d = gx_ref[rows, :] - x
+            col_ref[b, rows, :] = jnp.exp2(d * d * w).astype(BF16)
+
+    def add_window(s, low, row_ref, col_ref, lay_ref):
+        at = jnp.minimum(low, chunks - window)
+        rows = []
+        columns = []
+        for k in range(window):
+            mask = (lay_ref[at + k] == s) & (at + k >= low)
+            rows.append(row_ref[at + k])
+            columns.append(col_ref[at + k] * mask.astype(F32).astype(BF16))
+        acc_ref[s] += lax.dot_general(
+            jnp.concatenate(rows, axis=1),
+            jnp.concatenate(columns, axis=1),
+            (((1,), (1,)), ((), ())),
+            preferred_element_type=F32,
+        )
+
+    acc_ref[...] = jnp.zeros_like(acc_ref)
+    a_refs = (row_a, col_a, lay_a)
+    b_refs = (row_b, col_b, lay_b)
+    share = -(-chunks // layers)
+
+    def low_of(segment, s):
+        return bound_ref[segment, s] // LANES
+
+    def all_factors(segment, refs):
+        def one(b, carry):
+            factors(segment, b, *refs)
+            return carry
+
+        lax.fori_loop(0, chunks, one, 0)
+
+    def overlap(segment, refs, following, next_refs, over):
+        for s in range(layers):
+            low = low_of(segment, s)
+            add_window(s, low, *refs)
+            for b in range(s * share, min((s + 1) * share, chunks)):
+                factors(following, b, *next_refs)
+            over = jnp.maximum(over, bound_ref[segment, s + 1] - (low + window) * LANES)
+        return over
+
+    all_factors(0, a_refs)
+    over = jnp.int32(0)
+    last = segments - 1
+
+    def pair(i, over):
+        over = overlap(2 * i, a_refs, jnp.minimum(2 * i + 1, last), b_refs, over)
+        return overlap(2 * i + 1, b_refs, jnp.minimum(2 * i + 2, last), a_refs, over)
+
+    if segments > 1:
+        over = lax.fori_loop(0, segments // 2, pair, over)
+    else:
+        over = overlap(0, a_refs, 0, b_refs, over)
+
+    @pl.when(over > 0)
+    def _():
+        def segment_rest(segment, carry):
+            all_factors(segment, a_refs)
+
+            def slice_rest(s, carry):
+                low = low_of(segment, s)
+                chunk_end = (bound_ref[segment, s + 1] + LANES - 1) // LANES
+
+                def more(t, carry):
+                    add_window(s, low + t * window, *a_refs)
+                    return carry
+
+                return lax.fori_loop(1, (chunk_end - low + window - 1) // window, more, carry)
+
+            return lax.fori_loop(0, layers, slice_rest, carry)
+
+        lax.fori_loop(0, segments, segment_rest, 0)
+
+    for s in range(layers):
+        for r in range(0, G, 16):
+            rows = slice(r, r + 16)
+            out_ref[s, rows, :] = acc_ref[s, rows, :].astype(BF16)
+
+
+def build(plan, atoms, amps, widths, layers):
+    species = amps.shape[0]
+    count = atoms[0].shape[-1]
+    vmem = pl.BlockSpec(memory_space=pltpu.VMEM)
+    smem = pl.BlockSpec(memory_space=pltpu.SMEM)
+
+    def body(*refs):
+        build_body(layers, species, plan.n, *refs)
+
+    blocks = (count // LANES, G, LANES)
+    buffers = [pltpu.VMEM(blocks, BF16), pltpu.VMEM(blocks, BF16), pltpu.VMEM((count // LANES, 1, LANES), F32)]
+    return pl.pallas_call(
+        body,
+        out_shape=jax.ShapeDtypeStruct((layers, G, G), BF16),
+        in_specs=[smem, smem] + [vmem] * len(atoms),
+        out_specs=vmem,
+        scratch_shapes=[
+            pltpu.VMEM((G, LANES), F32),
+            pltpu.VMEM((G, LANES), F32),
+            pltpu.VMEM((layers, G, G), F32),
+            pltpu.VMEM((sum(a.shape[0] for a in atoms), 3, count), F32),
+            pltpu.SMEM((sum(a.shape[0] for a in atoms), layers + 1), jnp.int32),
+        ]
+        + buffers
+        + buffers,
         name="build",
-    )(amps, widths, jnp.asarray(grid_y), jnp.asarray(grid_x), atoms)
-
-
-def init_body(shift_ref, phase_ref, spec_ref, ty_ref, tx_ref, q2_ref, ap_ref, z_ref, prop_ref, a_ref, b_ref):
+    )(amps, widths, *atoms)
+
+
+def init_body(with_prop, *refs):
+    if with_prop:
+        shift_ref, phase_ref, spec_ref, ty_ref, tx_ref, q2_ref, ap_ref, z_ref, prop_ref, a_ref, b_ref = refs
+        for layer in range(prop_ref.shape[0]):
+            for r in range(0, q2_ref.shape[0], 16):
+                rows = slice(r, r + 16)
+                c, s = cos_sin(phase_ref[layer] * q2_ref[rows, :])
+                prop_ref[layer, 0, rows, :] = ap_ref[rows, :] * c
+                prop_ref[layer, 1, rows, :] = -(ap_ref[rows, :] * s)
+    else:
+        shift_ref, spec_ref, ty_ref, tx_ref, z_ref, a_ref, b_ref = refs
     n = spec_ref.shape[-1]
     positions = z_ref.shape[0]
-    for layer in range(prop_ref.shape[0]):
-        for r in range(0, q2_ref.shape[0], 16):
-            rows = slice(r, r + 16)
-            c, s = cos_sin(phase_ref[layer] * q2_ref[rows, :])
-            prop_ref[layer, 0, rows, :] = ap_ref[rows, :] * c
-            prop_ref[layer, 1, rows, :] = -(ap_ref[rows, :] * s)
     for p in range(positions):
         sy = shift_ref[p, 0]
         sx = shift_ref[p, 1]
@@ -235,25 +388,29 @@
     positions = shifts.shape[0]
     vmem = pl.BlockSpec(memory_space=pltpu.VMEM)
     smem = pl.BlockSpec(memory_space=pltpu.SMEM)
+    with_prop = slice_phase is not None
+    tables = (jnp.asarray(plan.start_y, BF16), jnp.asarray(plan.start_x, BF16))
+    waves = jax.ShapeDtypeStruct((positions, 2, n, n), F32)
+    if with_prop:
+        args = (shifts, slice_phase, spectrum, *tables, jnp.asarray(plan.q2), jnp.asarray(plan.aperture))
+        specs = [smem, smem, vmem, vmem, vmem, vmem, vmem]
+        out = (waves, jax.ShapeDtypeStruct((slice_phase.shape[0], 2, plan.rows, n), F32))
+    else:
+        args = (shifts, spectrum, *tables)
+        specs = [smem, vmem, vmem, vmem]
+        out = waves
+
+    def body(*refs):
+        init_body(with_prop, *refs)
+
     return pl.pallas_call(
-        init_body,
-        out_shape=(
-            jax.ShapeDtypeStruct((positions, 2, n, n), F32),
-            jax.ShapeDtypeStruct((slice_phase.shape[0], 2, plan.rows, n), F32),
-        ),
-        in_specs=[smem, smem, vmem, vmem, vmem, vmem, vmem],
-        out_specs=(vmem, vmem),
+        body,
+        out_shape=out,
+        in_specs=specs,
+        out_specs=(vmem, vmem) if with_prop else vmem,
         scratch_shapes=[pltpu.VMEM((positions, 2 * n, n), BF16), pltpu.VMEM((positions, n, 2 * n), BF16)],
         name="init",
-    )(
-        shifts,
-        slice_phase,
-        spectrum,
-        jnp.asarray(plan.start_y, BF16),
-        jnp.asarray(plan.start_x, BF16),
-        jnp.asarray(plan.q2),
-        jnp.asarray(plan.aperture),
-    )
+    )(*args)
 
 
 def halves(x, axis):
@@ -279,19 +436,38 @@
     return u.astype(BF16), w.astype(BF16)
 
 
-def slice_body(plan, direct, off_ref, own_ref, got_ref, z0_ref, prop_ref, fy_ref, fx_ref, iy_ref, ix_ref,
-               ly_ref, lx_ref, la_ref, out_ref, v_ref, z_ref, u_ref, y_ref, t_ref, x_ref, sem):
+def slice_body(plan, direct, off_ref, own_ref, got_ref, za_ref, zb_ref, prop_ref, fy_ref, fx_ref, iy_ref, ix_ref,
+               ly_ref, lx_ref, la_ref, out_ref, part_ref, v_ref, z_ref, u_ref, y_ref, t_ref, x_ref, sem, wave_sem):
     n = plan.n
     rows_f = plan.rows
-    positions = z0_ref.shape[0]
+    half = za_ref.shape[0]
+    positions = half + zb_ref.shape[0]
     layers = own_ref.shape[0]
-    fetch = pltpu.make_async_copy(z0_ref, z_ref, sem)
-    fetch.start()
+
+    def fetch(layer):
+        return [
+            pltpu.make_async_copy(own_ref.at[layer], part_ref.at[0, layer], sem.at[0, layer]),
+            pltpu.make_async_copy(got_ref.at[layer], part_ref.at[1, layer], sem.at[1, layer]),
+        ]
+
+    waves = [
+        pltpu.make_async_copy(za_ref, z_ref.at[:half], wave_sem.at[0]),
+        pltpu.make_async_copy(zb_ref, z_ref.at[half:], wave_sem.at[1]),
+    ]
+    for copy in fetch(0):
+        copy.start()
+    for copy in waves:
+        copy.start()
+    for layer in range(1, layers):
+        for copy in fetch(layer):
+            copy.start()
 
     def combine(layer):
+        for copy in fetch(layer):
+            copy.wait()
         for r in range(0, G, 16):
             rows = slice(r, r + 16)
-            total = own_ref[layer, rows, :] + got_ref[layer, rows, :].astype(F32)
+            total = part_ref[0, layer, rows, :].astype(F32) + part_ref[1, layer, rows, :].astype(F32)
             v_ref[rows, :] = total.astype(BF16).astype(F32)
 
     lane = lax.broadcasted_iota(jnp.int32, (16, n), 1)
@@ -343,7 +519,8 @@
             z_ref[p, 1] = dot(iy_ref[...], t_ref[p, rows_f : 2 * rows_f])
         return carry
 
-    fetch.wait()
+    for copy in waves:
+        copy.wait()
     lax.fori_loop(0, layers - 1, step, 0)
     combine(layers - 1)
     keep = plan.keep
@@ -379,9 +556,10 @@
 
 def multislice(plan, offsets, own, got, start, prop, direct):
     n = plan.n
-    positions = start.shape[0]
+    positions = offsets.shape[0]
     vmem = pl.BlockSpec(memory_space=pltpu.VMEM)
     smem = pl.BlockSpec(memory_space=pltpu.SMEM)
+    anywhere = pl.BlockSpec(memory_space=pl.ANY)
     shape = (n // 16, positions, 16, n) if direct else (positions, n, n)
     count = 2 * plan.keep
 
@@ -391,23 +569,25 @@
     return pl.pallas_call(
         body,
         out_shape=jax.ShapeDtypeStruct(shape, BF16),
-        in_specs=[smem, vmem, vmem, pl.BlockSpec(memory_space=pl.ANY)] + [vmem] * 8,
+        in_specs=[smem] + [anywhere] * 4 + [vmem] * 8,
         out_specs=vmem,
         scratch_shapes=[
+            pltpu.VMEM((2,) + own.shape, BF16),
             pltpu.VMEM((G, G), F32),
             pltpu.VMEM((positions, 2, n, n), F32),
             pltpu.VMEM((positions, 2, n, n), BF16),
             pltpu.VMEM((positions, 2, count, n), F32),
             pltpu.VMEM((positions, 2 * count, n), BF16),
             pltpu.VMEM((positions, 2 * count, n), F32),
-            pltpu.SemaphoreType.DMA,
+            pltpu.SemaphoreType.DMA((2, own.shape[0])),
+            pltpu.SemaphoreType.DMA((2,)),
         ],
         name="multislice",
     )(
         offsets,
         own,
         got,
-        start,
+        *start,
         prop,
         jnp.asarray(plan.fwd_y, BF16),
         jnp.asarray(plan.fwd_x, BF16),
@@ -441,19 +621,19 @@
     layers = slice_phase.shape[0] + 1
     plan = Plan(n)
     species = species_amp.shape[0]
-    atom_rows = atom_species.shape[0] // LANES
-    code = (atom_slice * species + atom_species).astype(F32).reshape(atom_rows, LANES)
-    atoms = jnp.concatenate([atom_positions.reshape(2 * atom_rows, LANES), code], axis=0)[None]
-    widths = -0.5 * math.log2(math.e) / (species_width * species_width)
+    atoms = sort_atoms(atom_positions, atom_species, atom_slice, layers, species)
     atoms = gather_atoms(atoms, devices)
-    own = build(plan, atoms, species_amp, widths, layers)
-    pairs = [(i, i ^ 1) for i in range(devices)]
-    got = lax.ppermute(own.astype(BF16), "probe", pairs)
     shifts = (probe_shifts + window_offsets) & (n - 1)
-    start, prop = init(plan, shifts, slice_phase, probe_spectrum)
+    half = shifts.shape[0] // 2
+    start_a, prop = init(plan, shifts[:half], slice_phase, probe_spectrum)
+    *atoms, start_a, prop = lax.optimization_barrier((*atoms, start_a, prop))
+    own = build(plan, atoms, species_amp, species_width, layers)
+    got = swap(own, 1, devices)
+    shifts, own = lax.optimization_barrier((shifts[half:], own))
+    start_b = init(plan, shifts, None, probe_spectrum)
     rows = n // devices
     direct = rows % 16 == 0
-    intensity = multislice(plan, window_offsets, own, got, start, prop, direct)
+    intensity = multislice(plan, window_offsets, own, got, (start_a, start_b), prop, direct)
     positions = window_offsets.shape[0]
     if direct:
         received = lax.all_to_all(intensity, "probe", split_axis=0, concat_axis=0, tiled=True)

time: 114 us -> 84.8 us (0.74)
  Pallas kernels: 65.8 us -> 46.8 us
  other arithmetic: 6.9 us -> 1.46 us
  blocking collectives: 21.1 us -> 18.7 us
  waiting for transfers between devices: 4.4 us -> 3.02 us
  local copies, waits for them, and re-layouts: 5.42 us -> 4.25 us
    pallas_call x2 -> x4, Pallas kernels: 47 us -> 28.6 us  [the longest x1 17.4 us: build(): pl.pallas_call(body, out_shape=jax.ShapeDtypeStruct((layers, G, G), BF16)...]
    convert_element_type x1 -> x0, other arithmetic: 3.8 us -> none  [on_device(): got = lax.ppermute(own.astype(BF16), 'probe', pairs)]
    another operation x2 -> x0, local copies, waits for them, and re-layouts: 3.03 us -> none
    all_to_all x1, blocking collectives: 21.1 us -> 18.7 us  [on_device(): lax.all_to_all(intensity, 'probe', split_axis=0, concat_axis=0, tiled=True)]
    unnamed x13, local copies, waits for them, and re-layouts: 1.69 us -> 3.67 us
    ppermute x4, waiting for transfers between devices: 4.4 us -> 3.02 us  [swap(): return lax.ppermute(block, 'probe', [(i, i ^ step) for i in range(devices)])]
    div x1 -> x0, other arithmetic: 1.14 us -> none  [on_device(): widths = -0.5 * math.log2(math.e) / (species_width * species_width)]
  transfers between devices with their start and end apart: 4 -> 4, of which waited for: 3 -> 3; matrix products, arithmetic and copies ran while one was open for 2% -> 3% of each run, Pallas kernels for 5% -> 9%
where the time goes in v2:
time: 84.8 us; the launch traced here: 84.2 us
  Pallas kernels  46.8 us (55%)
  blocking collectives  18.7 us (22%)
  starting transfers between devices  8.24 us (10%)
  local copies, waits for them, and re-layouts  4.25 us (5%)
  waiting for transfers between devices  3.02 us (4%)
  matrix products  1.73 us (2%)
  other arithmetic  1.46 us (2%)
    all_to_all x1, blocking collectives, on_device(): lax.all_to_all(intensity, 'probe', split_axis=0, concat_axis=0, tiled=True)  18.7 us
    pallas_call x1, Pallas kernels, multislice(): pl.pallas_call(body, out_shape=jax.ShapeDtypeStruct(shape, BF16), in_spec...  18.2 us
    pallas_call x1, Pallas kernels, build(): pl.pallas_call(body, out_shape=jax.ShapeDtypeStruct((layers, G, G), BF16)...  17.4 us
    ppermute x4, starting transfers between devices, swap(): return lax.ppermute(block, 'probe', [(i, i ^ step) for i in range(devices)])  8.24 us
    pallas_call x2, Pallas kernels, init(): pl.pallas_call(body, out_shape=out, in_specs=specs, out_specs=(vmem, vmem...  7.78 us
    unnamed x13, local copies, waits for them, and re-layouts  3.67 us
    pallas_call x1, Pallas kernels, sort_atoms(): pl.pallas_call(body, out_shape=jax.ShapeDtypeStruct((1, 3, count), F32),...  3.38 us
    ppermute x4, waiting for transfers between devices, swap(): return lax.ppermute(block, 'probe', [(i, i ^ step) for i in range(devices)])  3.02 us
  transfers between devices with their start and end apart: 4, of which 3 were waited for; matrix products, arithmetic and copies ran while one was open for 3% of the time, Pallas kernels for 9%

profile of v2, /device:TPU:0, one launch (start us, length us, event | category | flops | bytes accessed | tf_op | source)
XLA Modules:
  0.0 84.2 jit_solution(2570485008486371886)
XLA Ops:
  0.0 3.4 %sort.1 = f32[1,3,1024]{2,1,0:T(4,128)} custom-call(f32[2,1024]{1,0:T(2,128)} %refs_0_.3, s32[8,128]{1,0:T(8,128)} %bitcast.12, s32[8,128]{1,0:T(8,128)} %bitcast.14, s32[1,1024]{1,0:T(1,128)} %bitcast.13, s32[1,1024]{1,0:T(1,128)} %bitcast.15), custom_call_target="tpu_custom_call" | custom-call | tf_op jit(solution)/shard_map/sort/pallas_call | solution.py:182
  3.4 3.0 %collective-permute-start = (f32[1,3,1024]{2,1,0:T(4,128)}, f32[1,3,1024]{2,1,0:T(4,128)S(1)}, u32[]{:S(2)}, u32[]{:S(2)}) collective-permute-start(f32[1,3,1024]{2,1,0:T(4,128)} %sort.1), channel_id=1, source_target_pairs={{0,2},{1,3},{2,0},{3,1},{4,6},{5,7},{6,4},{7,5},{8,10},{9,11},{10,... | collective-permute-start | bytes 36872 | tf_op jit(solution)/shard_map/ppermute | solution.py:136
  6.4 0.8 copy.26.refs_0_
  7.1 0.0 copy-start.4
  7.1 0.8 copy.24
  7.9 0.4 collective-permute-done
  8.3 0.7 pad_maximum_fusion.1
  9.0 2.1 %collective-permute-start.1 = (f32[2,3,1024]{2,1,0:T(4,128)S(1)}, f32[2,3,1024]{2,1,0:T(4,128)S(1)}, u32[]{:S(2)}, u32[]{:S(2)}) collective-permute-start(f32[2,3,1024]{2,1,0:T(4,128)S(1)} %pad_maximum_fusion.1), channel_id=1, source_target_pairs={{0,4},{1,5},{2,6},{3,7},{4,0},{5,1},{6,2},{7,3},{8,12},{9,13},{10,... | collective-permute-start | bytes 73736 | tf_op jit(solution)/shard_map/ppermute | solution.py:136
  11.2 1.9 %collective-permute-done.1 = f32[2,3,1024]{2,1,0:T(4,128)S(1)} collective-permute-done((f32[2,3,1024]{2,1,0:T(4,128)S(1)}, f32[2,3,1024]{2,1,0:T(4,128)S(1)}, u32[]{:S(2)}, u32[]{:S(2)}) %collective-permute-start.1) | collective-permute-done | bytes 24608 | tf_op jit(solution)/shard_map/ppermute | solution.py:136
  13.1 0.7 pad_maximum_fusion.refs_2_
  13.8 0.0 copy-start.1
  13.8 3.1 %collective-permute-start.2 = (f32[4,3,1024]{2,1,0:T(4,128)S(1)}, f32[4,3,1024]{2,1,0:T(4,128)S(1)}, u32[]{:S(2)}, u32[]{:S(2)}) collective-permute-start(f32[4,3,1024]{2,1,0:T(4,128)S(1)} %pad_maximum_fusion.refs_2_), channel_id=1, source_target_pairs={{0,8},{1,9},{2,10},{3,11},{4,12},{5,13},{6,14},{7,15},{8,0},{9,1},... | collective-permute-start | bytes 147464 | tf_op jit(solution)/shard_map/ppermute | solution.py:136
  16.9 0.6 fusion
  17.5 4.1 %init.2 = (f32[2,2,256,256]{3,2,1,0:T(8,128)}, f32[3,2,176,256]{3,2,1,0:T(8,128)}) custom-call(s32[2,2]{1,0:T(2,128)} %get-tuple-element.21.refs_0_, f32[3]{0:T(128)} %refs_1_.3, f32[2,256,256]{2,1,0:T(8,128)} %refs_1_.5, bf16[2,256,512]{2,1,0:T(8,128)(2,1)} %constant.26.clone.refs_3_.refs_2_, bf16[2,512,256]{2,1,0:T(8,128)(2,1)} %constant.27.clone.refs_4_.refs_3_, ...), custom_call_target="tpu_custom_call" | custom-call | tf_op jit(solution)/shard_map/init/pallas_call | solution.py:406
  21.6 0.0 collective-permute-done.2.refs_3_
  21.6 0.0 copy-start.2
  21.7 0.0 copy-done.1
  21.7 0.6 copy-done.2
  22.3 17.4 %build.1.refs_1_ = bf16[4,512,512]{2,1,0:T(8,128)(2,1)} custom-call(f32[8]{0:T(128)} %refs_0_.4, f32[8]{0:T(128)} %refs_1_.4, f32[4,3,1024]{2,1,0:T(4,128)} %copy-done.1, f32[4,3,1024]{2,1,0:T(4,128)} %copy-done.2), custom_call_target="tpu_custom_call" | custom-call | tf_op jit(solution)/shard_map/build/pallas_call | solution.py:336
  39.7 0.0 copy-done.4
  39.7 0.0 collective-permute-start.3
  39.7 3.6 %init.3.refs_4_ = f32[2,2,256,256]{3,2,1,0:T(8,128)} custom-call(s32[2,2]{1,0:T(2,128)} %get-tuple-element.19.refs_0_, f32[2,256,256]{2,1,0:T(8,128)} %refs_1_.5, bf16[2,256,512]{2,1,0:T(8,128)(2,1)} %constant.26.clone.refs_3_.refs_2_, bf16[2,512,256]{2,1,0:T(8,128)(2,1)} %constant.27.clone.refs_4_.refs_3_), custom_call_target="tpu_custom_call" | custom-call | tf_op jit(solution)/shard_map/init/pallas_call | solution.py:406
  43.4 0.7 collective-permute-done.3.refs_2_
  44.1 0.0 copy-start
  44.1 1.3 %copy-done = bf16[4,512,512]{2,1,0:T(8,128)(2,1)} copy-done((bf16[4,512,512]{2,1,0:T(8,128)(2,1)}, bf16[4,512,512]{2,1,0:T(8,128)(2,1)S(1)}, u32[]{:S(2)}) %copy-start) | copy-done | bytes 2097176
  45.4 18.2 %multislice.1 = bf16[16,4,16,256]{3,2,1,0:T(8,128)(2,1)} custom-call(s32[4,2]{1,0:T(4,128)} %copy-done.4, bf16[4,512,512]{2,1,0:T(8,128)(2,1)} %build.1.refs_1_, bf16[4,512,512]{2,1,0:T(8,128)(2,1)} %copy-done, f32[2,2,256,256]{3,2,1,0:T(8,128)} %get-tuple-element.18.refs_3_, f32[2,2,256,256]{3,2,1,0:T(8,128)} %init.3.refs_4_, ...), custom_call_target="tpu_custom_call" | custom-call | tf_op jit(solution)/shard_map/multislice/pallas_call | solution.py:569
  63.6 0.0 copy-start.3
  63.6 18.7 %all_to_all.5 = bf16[16,4,16,256]{3,2,1,0:T(8,128)(2,1)S(1)} all-to-all(bf16[16,4,16,256]{3,2,1,0:T(8,128)(2,1)} %multislice.1), channel_id=1, replica_groups=mesh['groups'=2,'probe'=16] {'probe'}, dimensions={0} | all-to-all | bytes 1048576 | tf_op jit(solution)/shard_map/all_to_all | solution.py:639
  82.2 0.2 copy.27
  82.4 0.0 copy-done.3
  82.4 1.7 %fusion.1 = f32[128,4096]{1,0:T(8,128)} fusion(bf16[128,64]{1,0:T(8,128)(2,1)S(1)} %copy-done.3, bf16[64,4096]{1,0:T(8,128)(2,1)S(1)} %bitcast.11), kind=kOutput, calls=%fused_computation.4 | convolution fusion | flops 67108864 | bytes 2637824 | tf_op jit(solution)/shard_map/dot_general | solution.py:119
  (1 shorter events, 0.0 us)
Async XLA Ops:
  3.4 4.9 %collective-permute-start = (f32[1,3,1024]{2,1,0:T(4,128)}, f32[1,3,1024]{2,1,0:T(4,128)S(1)}, u32[]{:S(2)}, u32[]{:S(2)}) collective-permute-start(f32[1,3,1024]{2,1,0:T(4,128)} %sort.1), channel_id=1, source_target_pairs={{0,2},{1,3},{2,0},{3,1},{4,6},{5,7},{6,4},{7,5},{8,10},{9,11},{10,... | collective-permute-start | bytes 36872 | tf_op jit(solution)/shard_map/ppermute | solution.py:136
  7.1 32.6 %copy-start.4 = (s32[4,2]{1,0:T(4,128)}, s32[4,2]{1,0:T(4,128)S(1)}, u32[]{:S(2)}) copy-start(s32[4,2]{1,0:T(4,128)S(1)} %copy.26.refs_0_) | copy-start | bytes 100
  9.0 4.0 %collective-permute-start.1 = (f32[2,3,1024]{2,1,0:T(4,128)S(1)}, f32[2,3,1024]{2,1,0:T(4,128)S(1)}, u32[]{:S(2)}, u32[]{:S(2)}) collective-permute-start(f32[2,3,1024]{2,1,0:T(4,128)S(1)} %pad_maximum_fusion.1), channel_id=1, source_target_pairs={{0,4},{1,5},{2,6},{3,7},{4,0},{5,1},{6,2},{7,3},{8,12},{9,13},{10,... | collective-permute-start | bytes 73736 | tf_op jit(solution)/shard_map/ppermute | solution.py:136
  13.8 7.8 %copy-start.1 = (f32[4,3,1024]{2,1,0:T(4,128)}, f32[4,3,1024]{2,1,0:T(4,128)S(1)}, u32[]{:S(2)}) copy-start(f32[4,3,1024]{2,1,0:T(4,128)S(1)} %pad_maximum_fusion.refs_2_) | copy-start | bytes 147460
  13.8 7.8 %collective-permute-start.2 = (f32[4,3,1024]{2,1,0:T(4,128)S(1)}, f32[4,3,1024]{2,1,0:T(4,128)S(1)}, u32[]{:S(2)}, u32[]{:S(2)}) collective-permute-start(f32[4,3,1024]{2,1,0:T(4,128)S(1)} %pad_maximum_fusion.refs_2_), channel_id=1, source_target_pairs={{0,8},{1,9},{2,10},{3,11},{4,12},{5,13},{6,14},{7,15},{8,0},{9,1},... | collective-permute-start | bytes 147464 | tf_op jit(solution)/shard_map/ppermute | solution.py:136
  21.6 0.6 copy-start.2
  39.7 4.4 %collective-permute-start.3 = (bf16[4,512,512]{2,1,0:T(8,128)(2,1)}, bf16[4,512,512]{2,1,0:T(8,128)(2,1)S(1)}, u32[]{:S(2)}, u32[]{:S(2)}) collective-permute-start(bf16[4,512,512]{2,1,0:T(8,128)(2,1)} %build.1.refs_1_), channel_id=1, source_target_pairs={{0,1},{1,0},{2,3},{3,2},{4,5},{5,4},{6,7},{7,6},{8,9},{9,8},{10,11... | collective-permute-start | bytes 6291464 | tf_op jit(solution)/shard_map/ppermute | solution.py:136
  44.1 1.3 %copy-start = (bf16[4,512,512]{2,1,0:T(8,128)(2,1)}, bf16[4,512,512]{2,1,0:T(8,128)(2,1)S(1)}, u32[]{:S(2)}) copy-start(bf16[4,512,512]{2,1,0:T(8,128)(2,1)S(1)} %collective-permute-done.3.refs_2_) | copy-start | bytes 6291460
  63.6 18.9 %copy-start.3 = (bf16[128,64]{1,0:T(8,128)(2,1)S(1)}, bf16[128,64]{1,0:T(8,128)(2,1)}, u32[]{:S(2)}) copy-start(bf16[128,64]{1,0:T(8,128)(2,1)} %constant.37.clone) | copy-start | bytes 49156

commit v3 on v2

--- a/solution.py
+++ b/solution.py
@@ -161,15 +161,13 @@
             one_ref[slice(r, r + 16), slice(b * LANES, (b + 2) * LANES)] = hit
     code = (kind_row_ref[...] + species * layer_row_ref[...]).astype(F32)
     values = jnp.concatenate([pos_ref[...], code], axis=0)
-    high = values.astype(BF16)
-    rest = values - high.astype(F32)
-    middle = rest.astype(BF16)
-    low = (rest - middle.astype(F32)).astype(BF16)
-    parts = [
-        lax.dot_general(p, one_ref[...], (((1,), (1,)), ((), ())), preferred_element_type=F32)
-        for p in (high, middle, low)
-    ]
-    out_ref[0] = (parts[0] + parts[1]) + parts[2]
+    high = values.astype(BF16).astype(F32)
+    middle = (values - high).astype(BF16).astype(F32)
+    low = (values - high) - middle
+    parts = jnp.concatenate([high, middle, low], axis=0).astype(BF16)
+    moved = lax.dot_general(parts, one_ref[...], (((1,), (1,)), ((), ())), preferred_element_type=F32)
+    fields = values.shape[0]
+    out_ref[0] = (moved[:fields] + moved[fields : 2 * fields]) + moved[2 * fields :]
 
 
 def sort_atoms(positions, kind, layer, layers, species):
@@ -491,32 +489,60 @@
             u_ref[p, 0, rows, :] = u
             u_ref[p, 1, rows, :] = w
 
+    spans = [
+        (slice(16 * g, 16 * g + 16), slice(rows_f + 16 * g, rows_f + 16 * g + 16))
+        for g in range(rows_f // 16)
+    ]
+
+    def forward_rows(p, layer):
+        y_ref[p, 0, :rows_f] = dot(fy_ref[...], u_ref[p, 0])
+        y_ref[p, 1, :rows_f] = dot(fy_ref[...], u_ref[p, 1])
+
+    def pair_columns(p, layer):
+        for rows, low in spans:
+            t_ref[p, rows, :], t_ref[p, low, :] = forward_pair(y_ref[p, 0, rows, :], y_ref[p, 1, rows, :], 1)
+
+    def forward_columns(p, layer):
+        x_ref[p, : 2 * rows_f] = dot(t_ref[p, : 2 * rows_f], fx_ref[...])
+
+    def propagate(p, layer):
+        for rows, low in spans:
+            re = x_ref[p, rows, :]
+            im = x_ref[p, low, :]
+            pr = prop_ref[layer, 0, rows, :]
+            pi = prop_ref[layer, 1, rows, :]
+            t_ref[p, rows, :], t_ref[p, low, :] = inverse_pair(re * pr - im * pi, re * pi + im * pr, 1)
+
+    def inverse_columns(p, layer):
+        x_ref[p, : 2 * rows_f] = dot(t_ref[p, : 2 * rows_f], ix_ref[...])
+
+    def pair_rows(p, layer):
+        for rows, low in spans:
+            t_ref[p, rows, :], t_ref[p, low, :] = inverse_pair(x_ref[p, rows, :], x_ref[p, low, :], 0)
+
+    def inverse_rows(p, layer):
+        z_ref[p, 0] = dot(iy_ref[...], t_ref[p, :rows_f])
+        z_ref[p, 1] = dot(iy_ref[...], t_ref[p, rows_f : 2 * rows_f])
+
+    stages = [
+        lambda p, layer: transmit(p),
+        forward_rows,
+        pair_columns,
+        forward_columns,
+        propagate,
+        inverse_columns,
+        pair_rows,
+        inverse_rows,
+    ]
+    def in_turn(steps, layer):
+        for t in range(len(steps) + positions - 1):
+            for p in range(positions):
+                if 0 <= t - p < len(steps):
+                    steps[t - p](p, layer)
+
     def step(layer, carry):
         combine(layer)
-        for p in range(positions):
-            transmit(p)
-            y_ref[p, 0, :rows_f] = dot(fy_ref[...], u_ref[p, 0])
-            y_ref[p, 1, :rows_f] = dot(fy_ref[...], u_ref[p, 1])
-            for g in range(rows_f // 16):
-                rows = slice(16 * g, 16 * g + 16)
-                low = slice(rows_f + 16 * g, rows_f + 16 * g + 16)
-                t_ref[p, rows, :], t_ref[p, low, :] = forward_pair(y_ref[p, 0, rows, :], y_ref[p, 1, rows, :], 1)
-            x_ref[p, : 2 * rows_f] = dot(t_ref[p, : 2 * rows_f], fx_ref[...])
-            for g in range(rows_f // 16):
-                rows = slice(16 * g, 16 * g + 16)
-                low = slice(rows_f + 16 * g, rows_f + 16 * g + 16)
-                re = x_ref[p, rows, :]
-                im = x_ref[p, low, :]
-                pr = prop_ref[layer, 0, rows, :]
-                pi = prop_ref[layer, 1, rows, :]
-                t_ref[p, rows, :], t_ref[p, low, :] = inverse_pair(re * pr - im * pi, re * pi + im * pr, 1)
-            x_ref[p, : 2 * rows_f] = dot(t_ref[p, : 2 * rows_f], ix_ref[...])
-            for g in range(rows_f // 16):
-                rows = slice(16 * g, 16 * g + 16)
-                low = slice(rows_f + 16 * g, rows_f + 16 * g + 16)
-                t_ref[p, rows, :], t_ref[p, low, :] = inverse_pair(x_ref[p, rows, :], x_ref[p, low, :], 0)
-            z_ref[p, 0] = dot(iy_ref[...], t_ref[p, :rows_f])
-            z_ref[p, 1] = dot(iy_ref[...], t_ref[p, rows_f : 2 * rows_f])
+        in_turn(stages, layer)
         return carry
 
     for copy in waves:
@@ -524,22 +550,28 @@
     lax.fori_loop(0, layers - 1, step, 0)
     combine(layers - 1)
     keep = plan.keep
-    for p in range(positions):
-        transmit(p)
+    count = 2 * keep
+
+    def last_rows(p, layer):
         y_ref[p, 0] = dot(ly_ref[...], u_ref[p, 0])
         y_ref[p, 1] = dot(ly_ref[...], u_ref[p, 1])
-        count = 2 * keep
+
+    def last_pairs(p, layer):
         for g in range(count // 16):
             rows = slice(16 * g, 16 * g + 16)
             low = slice(count + 16 * g, count + 16 * g + 16)
             t_ref[p, rows, :], t_ref[p, low, :] = forward_pair(y_ref[p, 0, rows, :], y_ref[p, 1, rows, :], 1)
+
+    def last_columns(p, layer):
         x_ref[p] = dot(t_ref[p], lx_ref[...])
+
+    def intensity(p, layer):
         for g in range(n // 16):
             r = 16 * g
             if r < keep:
                 src = r
             elif r >= n - keep:
-                src = r - (n - 2 * keep)
+                src = r - (n - count)
             else:
                 src = None
             if src is None:
@@ -552,6 +584,8 @@
                 out_ref[g, p] = value
             else:
                 out_ref[p, slice(r, r + 16), :] = value
+
+    in_turn([stages[0], last_rows, last_pairs, last_columns, intensity], layers - 1)
 
 
 def multislice(plan, offsets, own, got, start, prop, direct):
@@ -624,7 +658,7 @@
     atoms = sort_atoms(atom_positions, atom_species, atom_slice, layers, species)
     atoms = gather_atoms(atoms, devices)
     shifts = (probe_shifts + window_offsets) & (n - 1)
-    half = shifts.shape[0] // 2
+    half = -(-shifts.shape[0] // 4)
     start_a, prop = init(plan, shifts[:half], slice_phase, probe_spectrum)
     *atoms, start_a, prop = lax.optimization_barrier((*atoms, start_a, prop))
     own = build(plan, atoms, species_amp, species_width, layers)

time: 84.8 us -> 80.9 us (0.954)
  Pallas kernels: 46.8 us -> 42.4 us
    pallas_call x1, Pallas kernels: 18.2 us -> 14.7 us  [multislice(): pl.pallas_call(body, out_shape=jax.ShapeDtypeStruct(shape, BF16), in_spec...]
    pallas_call x1, Pallas kernels: 3.38 us -> 2.31 us  [sort_atoms(): pl.pallas_call(body, out_shape=jax.ShapeDtypeStruct((1, 3, count), F32),...]
  transfers between devices with their start and end apart: 4 -> 4, of which waited for: 3 -> 2; matrix products, arithmetic and copies ran while one was open for 3% -> 3% of each run, Pallas kernels for 9% -> 10%
where the time goes in v3:
time: 80.9 us; the launch traced here: 80.3 us
  Pallas kernels  42.4 us (52%)
  blocking collectives  19.4 us (24%)
  starting transfers between devices  8.24 us (10%)
  local copies, waits for them, and re-layouts  4.77 us (6%)
  waiting for transfers between devices  2.29 us (3%)
  matrix products  1.73 us (2%)
  other arithmetic  1.46 us (2%)
    all_to_all x1, blocking collectives, on_device(): lax.all_to_all(intensity, 'probe', split_axis=0, concat_axis=0, tiled=True)  19.4 us
    pallas_call x1, Pallas kernels, build(): pl.pallas_call(body, out_shape=jax.ShapeDtypeStruct((layers, G, G), BF16)...  17.5 us
    pallas_call x1, Pallas kernels, multislice(): pl.pallas_call(body, out_shape=jax.ShapeDtypeStruct(shape, BF16), in_spec...  14.7 us
    ppermute x4, starting transfers between devices, swap(): return lax.ppermute(block, 'probe', [(i, i ^ step) for i in range(devices)])  8.24 us
    pallas_call x2, Pallas kernels, init(): pl.pallas_call(body, out_shape=out, in_specs=specs, out_specs=(vmem, vmem...  7.96 us
    unnamed x13, local copies, waits for them, and re-layouts  3.68 us
    pallas_call x1, Pallas kernels, sort_atoms(): pl.pallas_call(body, out_shape=jax.ShapeDtypeStruct((1, 3, count), F32),...  2.31 us
    ppermute x4, waiting for transfers between devices, swap(): return lax.ppermute(block, 'probe', [(i, i ^ step) for i in range(devices)])  2.29 us
  transfers between devices with their start and end apart: 4, of which 2 were waited for; matrix products, arithmetic and copies ran while one was open for 3% of the time, Pallas kernels for 10%

profile of v3, /device:TPU:0, one launch (start us, length us, event | category | flops | bytes accessed | tf_op | source)
XLA Modules:
  0.0 80.3 jit_solution(13337956279470593156)
XLA Ops:
  0.0 2.3 %sort.1 = f32[1,3,1024]{2,1,0:T(4,128)} custom-call(f32[2,1024]{1,0:T(2,128)} %refs_0_.3, s32[8,128]{1,0:T(8,128)} %bitcast.12, s32[8,128]{1,0:T(8,128)} %bitcast.14, s32[1,1024]{1,0:T(1,128)} %bitcast.13, s32[1,1024]{1,0:T(1,128)} %bitcast.15), custom_call_target="tpu_custom_call" | custom-call | tf_op jit(solution)/shard_map/sort/pallas_call | solution.py:180
  2.3 3.0 %collective-permute-start = (f32[1,3,1024]{2,1,0:T(4,128)}, f32[1,3,1024]{2,1,0:T(4,128)S(1)}, u32[]{:S(2)}, u32[]{:S(2)}) collective-permute-start(f32[1,3,1024]{2,1,0:T(4,128)} %sort.1), channel_id=1, source_target_pairs={{0,2},{1,3},{2,0},{3,1},{4,6},{5,7},{6,4},{7,5},{8,10},{9,11},{10,... | collective-permute-start | bytes 36872 | tf_op jit(solution)/shard_map/ppermute | solution.py:136
  5.3 1.9 %collective-permute-done = f32[1,3,1024]{2,1,0:T(4,128)S(1)} collective-permute-done((f32[1,3,1024]{2,1,0:T(4,128)}, f32[1,3,1024]{2,1,0:T(4,128)S(1)}, u32[]{:S(2)}, u32[]{:S(2)}) %collective-permute-start) | collective-permute-done | bytes 12320 | tf_op jit(solution)/shard_map/ppermute | solution.py:136
  7.2 0.7 pad_maximum_fusion.1
  8.0 2.1 %collective-permute-start.1 = (f32[2,3,1024]{2,1,0:T(4,128)S(1)}, f32[2,3,1024]{2,1,0:T(4,128)S(1)}, u32[]{:S(2)}, u32[]{:S(2)}) collective-permute-start(f32[2,3,1024]{2,1,0:T(4,128)S(1)} %pad_maximum_fusion.1), channel_id=1, source_target_pairs={{0,4},{1,5},{2,6},{3,7},{4,0},{5,1},{6,2},{7,3},{8,12},{9,13},{10,... | collective-permute-start | bytes 73736 | tf_op jit(solution)/shard_map/ppermute | solution.py:136
  10.1 0.8 copy.26.refs_0_
  10.9 0.0 copy-start.4
  10.9 0.8 copy.24
  11.6 0.4 collective-permute-done.1
  12.0 0.7 pad_maximum_fusion.refs_2_
  12.7 0.0 copy-start.1
  12.7 3.1 %collective-permute-start.2 = (f32[4,3,1024]{2,1,0:T(4,128)S(1)}, f32[4,3,1024]{2,1,0:T(4,128)S(1)}, u32[]{:S(2)}, u32[]{:S(2)}) collective-permute-start(f32[4,3,1024]{2,1,0:T(4,128)S(1)} %pad_maximum_fusion.refs_2_), channel_id=1, source_target_pairs={{0,8},{1,9},{2,10},{3,11},{4,12},{5,13},{6,14},{7,15},{8,0},{9,1},... | collective-permute-start | bytes 147464 | tf_op jit(solution)/shard_map/ppermute | solution.py:136
  15.8 0.5 slice.7.refs_0_
  16.4 3.6 %init.2 = (f32[1,2,256,256]{3,2,1,0:T(8,128)}, f32[3,2,176,256]{3,2,1,0:T(8,128)}) custom-call(s32[1,2]{1,0:T(1,128)} %slice.7.refs_0_, f32[3]{0:T(128)} %refs_1_.3, f32[2,256,256]{2,1,0:T(8,128)} %refs_1_.5, bf16[2,256,512]{2,1,0:T(8,128)(2,1)} %constant.26.clone.refs_3_.refs_2_, bf16[2,512,256]{2,1,0:T(8,128)(2,1)} %constant.27.clone.refs_4_.refs_3_, ...), custom_call_target="tpu_custom_call" | custom-call | tf_op jit(solution)/shard_map/init/pallas_call | solution.py:404
  20.0 0.0 collective-permute-done.2.refs_3_
  20.0 0.0 copy-start.2
  20.0 0.0 copy-done.1
  20.0 0.6 copy-done.2
  20.6 17.5 %build.1.refs_1_ = bf16[4,512,512]{2,1,0:T(8,128)(2,1)} custom-call(f32[8]{0:T(128)} %refs_0_.4, f32[8]{0:T(128)} %refs_1_.4, f32[4,3,1024]{2,1,0:T(4,128)} %copy-done.1, f32[4,3,1024]{2,1,0:T(4,128)} %copy-done.2), custom_call_target="tpu_custom_call" | custom-call | tf_op jit(solution)/shard_map/build/pallas_call | solution.py:334
  38.1 0.0 copy-done.4
  38.1 0.0 collective-permute-start.3
  38.1 0.6 slice.6.refs_0_
  38.6 4.3 %init.3.refs_4_ = f32[3,2,256,256]{3,2,1,0:T(8,128)} custom-call(s32[3,2]{1,0:T(4,128)} %slice.6.refs_0_, f32[2,256,256]{2,1,0:T(8,128)} %refs_1_.5, bf16[2,256,512]{2,1,0:T(8,128)(2,1)} %constant.26.clone.refs_3_.refs_2_, bf16[2,512,256]{2,1,0:T(8,128)(2,1)} %constant.27.clone.refs_4_.refs_3_), custom_call_target="tpu_custom_call" | custom-call | tf_op jit(solution)/shard_map/init/pallas_call | solution.py:404
  43.0 0.0 collective-permute-done.3.refs_2_
  43.0 0.0 copy-start
  43.0 1.3 %copy-done = bf16[4,512,512]{2,1,0:T(8,128)(2,1)} copy-done((bf16[4,512,512]{2,1,0:T(8,128)(2,1)}, bf16[4,512,512]{2,1,0:T(8,128)(2,1)S(1)}, u32[]{:S(2)}) %copy-start) | copy-done | bytes 2097176
  44.3 14.7 %multislice.1 = bf16[16,4,16,256]{3,2,1,0:T(8,128)(2,1)} custom-call(s32[4,2]{1,0:T(4,128)} %copy-done.4, bf16[4,512,512]{2,1,0:T(8,128)(2,1)} %build.1.refs_1_, bf16[4,512,512]{2,1,0:T(8,128)(2,1)} %copy-done, f32[1,2,256,256]{3,2,1,0:T(8,128)} %get-tuple-element.18.refs_3_, f32[3,2,256,256]{3,2,1,0:T(8,128)} %init.3.refs_4_, ...), custom_call_target="tpu_custom_call" | custom-call | tf_op jit(solution)/shard_map/multislice/pallas_call | solution.py:603
  59.1 0.0 copy-start.3
  59.1 19.4 %all_to_all.5 = bf16[16,4,16,256]{3,2,1,0:T(8,128)(2,1)S(1)} all-to-all(bf16[16,4,16,256]{3,2,1,0:T(8,128)(2,1)} %multislice.1), channel_id=1, replica_groups=mesh['groups'=2,'probe'=16] {'probe'}, dimensions={0} | all-to-all | bytes 1048576 | tf_op jit(solution)/shard_map/all_to_all | solution.py:673
  78.4 0.2 copy.27
  78.6 0.0 copy-done.3
  78.6 1.7 %fusion = f32[128,4096]{1,0:T(8,128)} fusion(bf16[128,64]{1,0:T(8,128)(2,1)S(1)} %copy-done.3, bf16[64,4096]{1,0:T(8,128)(2,1)S(1)} %bitcast.11), kind=kOutput, calls=%fused_computation.3 | convolution fusion | flops 67108864 | bytes 2637824 | tf_op jit(solution)/shard_map/dot_general | solution.py:119
  (1 shorter events, 0.0 us)
Async XLA Ops:
  2.3 4.9 %collective-permute-start = (f32[1,3,1024]{2,1,0:T(4,128)}, f32[1,3,1024]{2,1,0:T(4,128)S(1)}, u32[]{:S(2)}, u32[]{:S(2)}) collective-permute-start(f32[1,3,1024]{2,1,0:T(4,128)} %sort.1), channel_id=1, source_target_pairs={{0,2},{1,3},{2,0},{3,1},{4,6},{5,7},{6,4},{7,5},{8,10},{9,11},{10,... | collective-permute-start | bytes 36872 | tf_op jit(solution)/shard_map/ppermute | solution.py:136
  8.0 4.0 %collective-permute-start.1 = (f32[2,3,1024]{2,1,0:T(4,128)S(1)}, f32[2,3,1024]{2,1,0:T(4,128)S(1)}, u32[]{:S(2)}, u32[]{:S(2)}) collective-permute-start(f32[2,3,1024]{2,1,0:T(4,128)S(1)} %pad_maximum_fusion.1), channel_id=1, source_target_pairs={{0,4},{1,5},{2,6},{3,7},{4,0},{5,1},{6,2},{7,3},{8,12},{9,13},{10,... | collective-permute-start | bytes 73736 | tf_op jit(solution)/shard_map/ppermute | solution.py:136
  10.9 27.2 %copy-start.4 = (s32[4,2]{1,0:T(4,128)}, s32[4,2]{1,0:T(4,128)S(1)}, u32[]{:S(2)}) copy-start(s32[4,2]{1,0:T(4,128)S(1)} %copy.26.refs_0_) | copy-start | bytes 100
  12.7 7.3 %copy-start.1 = (f32[4,3,1024]{2,1,0:T(4,128)}, f32[4,3,1024]{2,1,0:T(4,128)S(1)}, u32[]{:S(2)}) copy-start(f32[4,3,1024]{2,1,0:T(4,128)S(1)} %pad_maximum_fusion.refs_2_) | copy-start | bytes 147460
  12.7 7.2 %collective-permute-start.2 = (f32[4,3,1024]{2,1,0:T(4,128)S(1)}, f32[4,3,1024]{2,1,0:T(4,128)S(1)}, u32[]{:S(2)}, u32[]{:S(2)}) collective-permute-start(f32[4,3,1024]{2,1,0:T(4,128)S(1)} %pad_maximum_fusion.refs_2_), channel_id=1, source_target_pairs={{0,8},{1,9},{2,10},{3,11},{4,12},{5,13},{6,14},{7,15},{8,0},{9,1},... | collective-permute-start | bytes 147464 | tf_op jit(solution)/shard_map/ppermute | solution.py:136
  20.0 0.6 copy-start.2
  38.1 4.9 %collective-permute-start.3 = (bf16[4,512,512]{2,1,0:T(8,128)(2,1)}, bf16[4,512,512]{2,1,0:T(8,128)(2,1)S(1)}, u32[]{:S(2)}, u32[]{:S(2)}) collective-permute-start(bf16[4,512,512]{2,1,0:T(8,128)(2,1)} %build.1.refs_1_), channel_id=1, source_target_pairs={{0,1},{1,0},{2,3},{3,2},{4,5},{5,4},{6,7},{7,6},{8,9},{9,8},{10,11... | collective-permute-start | bytes 6291464 | tf_op jit(solution)/shard_map/ppermute | solution.py:136
  43.0 1.3 %copy-start = (bf16[4,512,512]{2,1,0:T(8,128)(2,1)}, bf16[4,512,512]{2,1,0:T(8,128)(2,1)S(1)}, u32[]{:S(2)}) copy-start(bf16[4,512,512]{2,1,0:T(8,128)(2,1)S(1)} %collective-permute-done.3.refs_2_) | copy-start | bytes 6291460
  59.1 19.5 %copy-start.3 = (bf16[128,64]{1,0:T(8,128)(2,1)S(1)}, bf16[128,64]{1,0:T(8,128)(2,1)}, u32[]{:S(2)}) copy-start(bf16[128,64]{1,0:T(8,128)(2,1)} %constant.37.clone) | copy-start | bytes 49156

commit v4 on v3

--- a/solution.py
+++ b/solution.py
@@ -362,7 +362,8 @@
         shift_ref, spec_ref, ty_ref, tx_ref, z_ref, a_ref, b_ref = refs
     n = spec_ref.shape[-1]
     positions = z_ref.shape[0]
-    for p in range(positions):
+
+    def phases(p):
         sy = shift_ref[p, 0]
         sx = shift_ref[p, 1]
         for r in range(0, n, 16):
@@ -375,10 +376,20 @@
             im = spec_ref[1, rows, :]
             a_ref[p, rows, :] = (re * c + im * s).astype(BF16)
             a_ref[p, slice(n + r, n + r + 16), :] = (im * c - re * s).astype(BF16)
+
+    def along_y(p):
         b_ref[p, :, :n] = dot(ty_ref[0], a_ref[p]).astype(BF16)
         b_ref[p, :, n:] = dot(ty_ref[1], a_ref[p]).astype(BF16)
+
+    def along_x(p):
         z_ref[p, 0] = dot(b_ref[p], tx_ref[0])
         z_ref[p, 1] = dot(b_ref[p], tx_ref[1])
+
+    steps = [phases, along_y, along_x]
+    for t in range(len(steps) + positions - 1):
+        for p in range(positions):
+            if 0 <= t - p < len(steps):
+                steps[t - p](p)
 
 
 def init(plan, shifts, slice_phase, spectrum):

time: 80.9 us -> 80.9 us (level)
  no operation moved by 1% of the time
where the time goes in v4:
time: 80.9 us; the launch traced here: 80.3 us
  Pallas kernels  42.4 us (52%)
  blocking collectives  19.4 us (24%)
  starting transfers between devices  8.24 us (10%)
  local copies, waits for them, and re-layouts  4.77 us (6%)
  waiting for transfers between devices  2.29 us (3%)
  matrix products  1.73 us (2%)
  other arithmetic  1.46 us (2%)
    all_to_all x1, blocking collectives, on_device(): lax.all_to_all(intensity, 'probe', split_axis=0, concat_axis=0, tiled=True)  19.4 us
    pallas_call x1, Pallas kernels, build(): pl.pallas_call(body, out_shape=jax.ShapeDtypeStruct((layers, G, G), BF16)...  17.5 us
    pallas_call x1, Pallas kernels, multislice(): pl.pallas_call(body, out_shape=jax.ShapeDtypeStruct(shape, BF16), in_spec...  14.7 us
    ppermute x4, starting transfers between devices, swap(): return lax.ppermute(block, 'probe', [(i, i ^ step) for i in range(devices)])  8.24 us
    pallas_call x2, Pallas kernels, init(): pl.pallas_call(body, out_shape=out, in_specs=specs, out_specs=(vmem, vmem...  7.96 us
    unnamed x13, local copies, waits for them, and re-layouts  3.68 us
    pallas_call x1, Pallas kernels, sort_atoms(): pl.pallas_call(body, out_shape=jax.ShapeDtypeStruct((1, 3, count), F32),...  2.31 us
    ppermute x4, waiting for transfers between devices, swap(): return lax.ppermute(block, 'probe', [(i, i ^ step) for i in range(devices)])  2.29 us
  transfers between devices with their start and end apart: 4, of which 2 were waited for; matrix products, arithmetic and copies ran while one was open for 3% of the time, Pallas kernels for 10%

profile of v4, /device:TPU:0, one launch (start us, length us, event | category | flops | bytes accessed | tf_op | source)
XLA Modules:
  0.0 80.3 jit_solution(13337956279470593156)
XLA Ops:
  0.0 2.3 %sort.1 = f32[1,3,1024]{2,1,0:T(4,128)} custom-call(f32[2,1024]{1,0:T(2,128)} %refs_0_.3, s32[8,128]{1,0:T(8,128)} %bitcast.12, s32[8,128]{1,0:T(8,128)} %bitcast.14, s32[1,1024]{1,0:T(1,128)} %bitcast.13, s32[1,1024]{1,0:T(1,128)} %bitcast.15), custom_call_target="tpu_custom_call" | custom-call | tf_op jit(solution)/shard_map/sort/pallas_call | solution.py:180
  2.3 3.0 %collective-permute-start = (f32[1,3,1024]{2,1,0:T(4,128)}, f32[1,3,1024]{2,1,0:T(4,128)S(1)}, u32[]{:S(2)}, u32[]{:S(2)}) collective-permute-start(f32[1,3,1024]{2,1,0:T(4,128)} %sort.1), channel_id=1, source_target_pairs={{0,2},{1,3},{2,0},{3,1},{4,6},{5,7},{6,4},{7,5},{8,10},{9,11},{10,... | collective-permute-start | bytes 36872 | tf_op jit(solution)/shard_map/ppermute | solution.py:136
  5.3 1.9 %collective-permute-done = f32[1,3,1024]{2,1,0:T(4,128)S(1)} collective-permute-done((f32[1,3,1024]{2,1,0:T(4,128)}, f32[1,3,1024]{2,1,0:T(4,128)S(1)}, u32[]{:S(2)}, u32[]{:S(2)}) %collective-permute-start) | collective-permute-done | bytes 12320 | tf_op jit(solution)/shard_map/ppermute | solution.py:136
  7.2 0.7 pad_maximum_fusion.1
  8.0 2.1 %collective-permute-start.1 = (f32[2,3,1024]{2,1,0:T(4,128)S(1)}, f32[2,3,1024]{2,1,0:T(4,128)S(1)}, u32[]{:S(2)}, u32[]{:S(2)}) collective-permute-start(f32[2,3,1024]{2,1,0:T(4,128)S(1)} %pad_maximum_fusion.1), channel_id=1, source_target_pairs={{0,4},{1,5},{2,6},{3,7},{4,0},{5,1},{6,2},{7,3},{8,12},{9,13},{10,... | collective-permute-start | bytes 73736 | tf_op jit(solution)/shard_map/ppermute | solution.py:136
  10.1 0.8 copy.26.refs_0_
  10.9 0.0 copy-start.4
  10.9 0.8 copy.24
  11.6 0.4 collective-permute-done.1
  12.0 0.7 pad_maximum_fusion.refs_2_
  12.7 0.0 copy-start.1
  12.7 3.1 %collective-permute-start.2 = (f32[4,3,1024]{2,1,0:T(4,128)S(1)}, f32[4,3,1024]{2,1,0:T(4,128)S(1)}, u32[]{:S(2)}, u32[]{:S(2)}) collective-permute-start(f32[4,3,1024]{2,1,0:T(4,128)S(1)} %pad_maximum_fusion.refs_2_), channel_id=1, source_target_pairs={{0,8},{1,9},{2,10},{3,11},{4,12},{5,13},{6,14},{7,15},{8,0},{9,1},... | collective-permute-start | bytes 147464 | tf_op jit(solution)/shard_map/ppermute | solution.py:136
  15.8 0.5 slice.7.refs_0_
  16.4 3.6 %init.2 = (f32[1,2,256,256]{3,2,1,0:T(8,128)}, f32[3,2,176,256]{3,2,1,0:T(8,128)}) custom-call(s32[1,2]{1,0:T(1,128)} %slice.7.refs_0_, f32[3]{0:T(128)} %refs_1_.3, f32[2,256,256]{2,1,0:T(8,128)} %refs_1_.5, bf16[2,256,512]{2,1,0:T(8,128)(2,1)} %constant.26.clone.refs_3_.refs_2_, bf16[2,512,256]{2,1,0:T(8,128)(2,1)} %constant.27.clone.refs_4_.refs_3_, ...), custom_call_target="tpu_custom_call" | custom-call | tf_op jit(solution)/shard_map/init/pallas_call | solution.py:415
  20.0 0.0 collective-permute-done.2.refs_3_
  20.0 0.0 copy-start.2
  20.0 0.0 copy-done.1
  20.0 0.6 copy-done.2
  20.6 17.5 %build.1.refs_1_ = bf16[4,512,512]{2,1,0:T(8,128)(2,1)} custom-call(f32[8]{0:T(128)} %refs_0_.4, f32[8]{0:T(128)} %refs_1_.4, f32[4,3,1024]{2,1,0:T(4,128)} %copy-done.1, f32[4,3,1024]{2,1,0:T(4,128)} %copy-done.2), custom_call_target="tpu_custom_call" | custom-call | tf_op jit(solution)/shard_map/build/pallas_call | solution.py:334
  38.1 0.0 copy-done.4
  38.1 0.0 collective-permute-start.3
  38.1 0.6 slice.6.refs_0_
  38.6 4.3 %init.3.refs_4_ = f32[3,2,256,256]{3,2,1,0:T(8,128)} custom-call(s32[3,2]{1,0:T(4,128)} %slice.6.refs_0_, f32[2,256,256]{2,1,0:T(8,128)} %refs_1_.5, bf16[2,256,512]{2,1,0:T(8,128)(2,1)} %constant.26.clone.refs_3_.refs_2_, bf16[2,512,256]{2,1,0:T(8,128)(2,1)} %constant.27.clone.refs_4_.refs_3_), custom_call_target="tpu_custom_call" | custom-call | tf_op jit(solution)/shard_map/init/pallas_call | solution.py:415
  43.0 0.0 collective-permute-done.3.refs_2_
  43.0 0.0 copy-start
  43.0 1.3 %copy-done = bf16[4,512,512]{2,1,0:T(8,128)(2,1)} copy-done((bf16[4,512,512]{2,1,0:T(8,128)(2,1)}, bf16[4,512,512]{2,1,0:T(8,128)(2,1)S(1)}, u32[]{:S(2)}) %copy-start) | copy-done | bytes 2097176
  44.3 14.7 %multislice.1 = bf16[16,4,16,256]{3,2,1,0:T(8,128)(2,1)} custom-call(s32[4,2]{1,0:T(4,128)} %copy-done.4, bf16[4,512,512]{2,1,0:T(8,128)(2,1)} %build.1.refs_1_, bf16[4,512,512]{2,1,0:T(8,128)(2,1)} %copy-done, f32[1,2,256,256]{3,2,1,0:T(8,128)} %get-tuple-element.18.refs_3_, f32[3,2,256,256]{3,2,1,0:T(8,128)} %init.3.refs_4_, ...), custom_call_target="tpu_custom_call" | custom-call | tf_op jit(solution)/shard_map/multislice/pallas_call | solution.py:614
  59.1 0.0 copy-start.3
  59.1 19.4 %all_to_all.5 = bf16[16,4,16,256]{3,2,1,0:T(8,128)(2,1)S(1)} all-to-all(bf16[16,4,16,256]{3,2,1,0:T(8,128)(2,1)} %multislice.1), channel_id=1, replica_groups=mesh['groups'=2,'probe'=16] {'probe'}, dimensions={0} | all-to-all | bytes 1048576 | tf_op jit(solution)/shard_map/all_to_all | solution.py:684
  78.4 0.2 copy.27
  78.6 0.0 copy-done.3
  78.6 1.7 %fusion = f32[128,4096]{1,0:T(8,128)} fusion(bf16[128,64]{1,0:T(8,128)(2,1)S(1)} %copy-done.3, bf16[64,4096]{1,0:T(8,128)(2,1)S(1)} %bitcast.11), kind=kOutput, calls=%fused_computation.3 | convolution fusion | flops 67108864 | bytes 2637824 | tf_op jit(solution)/shard_map/dot_general | solution.py:119
  (1 shorter events, 0.0 us)
Async XLA Ops:
  2.3 4.9 %collective-permute-start = (f32[1,3,1024]{2,1,0:T(4,128)}, f32[1,3,1024]{2,1,0:T(4,128)S(1)}, u32[]{:S(2)}, u32[]{:S(2)}) collective-permute-start(f32[1,3,1024]{2,1,0:T(4,128)} %sort.1), channel_id=1, source_target_pairs={{0,2},{1,3},{2,0},{3,1},{4,6},{5,7},{6,4},{7,5},{8,10},{9,11},{10,... | collective-permute-start | bytes 36872 | tf_op jit(solution)/shard_map/ppermute | solution.py:136
  8.0 4.0 %collective-permute-start.1 = (f32[2,3,1024]{2,1,0:T(4,128)S(1)}, f32[2,3,1024]{2,1,0:T(4,128)S(1)}, u32[]{:S(2)}, u32[]{:S(2)}) collective-permute-start(f32[2,3,1024]{2,1,0:T(4,128)S(1)} %pad_maximum_fusion.1), channel_id=1, source_target_pairs={{0,4},{1,5},{2,6},{3,7},{4,0},{5,1},{6,2},{7,3},{8,12},{9,13},{10,... | collective-permute-start | bytes 73736 | tf_op jit(solution)/shard_map/ppermute | solution.py:136
  10.9 27.2 %copy-start.4 = (s32[4,2]{1,0:T(4,128)}, s32[4,2]{1,0:T(4,128)S(1)}, u32[]{:S(2)}) copy-start(s32[4,2]{1,0:T(4,128)S(1)} %copy.26.refs_0_) | copy-start | bytes 100
  12.7 7.3 %copy-start.1 = (f32[4,3,1024]{2,1,0:T(4,128)}, f32[4,3,1024]{2,1,0:T(4,128)S(1)}, u32[]{:S(2)}) copy-start(f32[4,3,1024]{2,1,0:T(4,128)S(1)} %pad_maximum_fusion.refs_2_) | copy-start | bytes 147460
  12.7 7.2 %collective-permute-start.2 = (f32[4,3,1024]{2,1,0:T(4,128)S(1)}, f32[4,3,1024]{2,1,0:T(4,128)S(1)}, u32[]{:S(2)}, u32[]{:S(2)}) collective-permute-start(f32[4,3,1024]{2,1,0:T(4,128)S(1)} %pad_maximum_fusion.refs_2_), channel_id=1, source_target_pairs={{0,8},{1,9},{2,10},{3,11},{4,12},{5,13},{6,14},{7,15},{8,0},{9,1},... | collective-permute-start | bytes 147464 | tf_op jit(solution)/shard_map/ppermute | solution.py:136
  20.0 0.6 copy-start.2
  38.1 4.9 %collective-permute-start.3 = (bf16[4,512,512]{2,1,0:T(8,128)(2,1)}, bf16[4,512,512]{2,1,0:T(8,128)(2,1)S(1)}, u32[]{:S(2)}, u32[]{:S(2)}) collective-permute-start(bf16[4,512,512]{2,1,0:T(8,128)(2,1)} %build.1.refs_1_), channel_id=1, source_target_pairs={{0,1},{1,0},{2,3},{3,2},{4,5},{5,4},{6,7},{7,6},{8,9},{9,8},{10,11... | collective-permute-start | bytes 6291464 | tf_op jit(solution)/shard_map/ppermute | solution.py:136
  43.0 1.3 %copy-start = (bf16[4,512,512]{2,1,0:T(8,128)(2,1)}, bf16[4,512,512]{2,1,0:T(8,128)(2,1)S(1)}, u32[]{:S(2)}) copy-start(bf16[4,512,512]{2,1,0:T(8,128)(2,1)S(1)} %collective-permute-done.3.refs_2_) | copy-start | bytes 6291460
  59.1 19.5 %copy-start.3 = (bf16[128,64]{1,0:T(8,128)(2,1)S(1)}, bf16[128,64]{1,0:T(8,128)(2,1)}, u32[]{:S(2)}) copy-start(bf16[128,64]{1,0:T(8,128)(2,1)} %constant.37.clone) | copy-start | bytes 49156
